TPU v7x, 32 devices: a whole 2x2x4 slice. The times are simulated.
32 devices in a mesh: edge: 4 (over y, x), tile: 8 (over z, core).
Axes of the slice: x: 2, y: 2, z: 4, core: 2. Of those that a mesh axis runs over, the one named last changes fastest.
Arguments:
- features: bfloat16 [96, 48, 64, 128], P('edge', 'tile'), may hold values from -6 to 6
- hidden_state: bfloat16 [32, 48, 64, 128], P('edge', 'tile'), may hold values from -1 to 1
- edge_source: int32 [32], P('edge'), may hold values from 0 to 23
- edge_owner: int32 [32, 1], P('edge'), may hold values from 0 to 3; in each aligned block of 8 rows (0 to 7, 8 to 15, ...) at most 4 rows name the same one
- edge_target: int32 [32], P('edge'), may hold values from 0 to 23
- edge_counts: int32 [4], P('edge'), may hold values from 4 to 8, as said below
- corr_weight: bfloat16 [49, 128], replicated, may hold values from -0.875 to 0.875
- gate_weight: bfloat16 [3, 3, 256, 256], replicated, may hold values from -0.125 to 0.125
- candidate_weight: bfloat16 [3, 3, 256, 128], replicated, may hold values from -0.125 to 0.125
- jacobian_weight: bfloat16 [128, 24], replicated, may hold values from -0.5 to 0.5
- confidence_weight: bfloat16 [128, 2], replicated, may hold values from -3 to 3
Outputs:
- hidden_next: bfloat16 [32, 48, 64, 128], P('edge', 'tile')
- camera_hessian: float32 [576, 576], P('tile', 'edge')
- pose_diagonal: float32 [96, 36], P('edge')
Inputs may be any that keep to these rules, and one draw needn't show every extreme that they name: `edge_owner`: in the rows of one index of edge at most 4 edges name the same owner, a bound that some block reaches. `edge_counts`: edges past a device's count are unused; some index of edge uses all 8.
All inputs are finite; a program needn't handle non-finite values.
Results may differ from a plain program's by a relative error of at most 0.015.
Values may be sent and summed in bfloat16 or wider, within the bound.
A program may use at most 128 MiB of HBM per device.

v0:
```python
import functools

import jax
import jax.numpy as jnp
from jax import lax
from jax.experimental import pallas as pl
from jax.experimental.pallas import tpu as pltpu
from jax.sharding import PartitionSpec as P

MAPH = 48
WINDOW = 7
RADIUS = WINDOW // 2
MESH = pl.DeviceIdType.MESH
HIGH = lax.Precision.HIGHEST
BF = jnp.bfloat16
F32 = jnp.float32


def nt(a, b, precision=None):
    return lax.dot_general(
        a, b, (((1,), (1,)), ((), ())), preferred_element_type=F32, precision=precision
    )


def nn(a, b, precision=None):
    return lax.dot_general(
        a, b, (((1,), (0,)), ((), ())), preferred_element_type=F32, precision=precision
    )


def iota(shape, dim):
    return lax.broadcasted_iota(jnp.int32, shape, dim)


def sixth(index):
    return jnp.floor((index.astype(F32) + 0.5) * (1.0 / 6.0))


def kernel(
    dims,
    meta_in,
    feat_h,
    hidden_h,
    corr_in,
    gate_w,
    cand_w,
    jac_in,
    conf_in,
    out_hidden,
    gall,
    meta_all,
    feat,
    held,
    l_out,
    corr_w,
    jall,
    wall,
    meta_s,
    send,
    text,
    sref,
    hext,
    mext,
    rext,
    x3,
    wh,
    wm,
    wr,
    gpre,
    cpre,
    upd,
    gpart,
    gtile,
    gsum,
    l_in,
    l_w,
    s_meta,
    r_meta,
    l_meta,
    s_feat,
    r_feat,
    s_tup,
    r_tup,
    s_tdn,
    r_tdn,
    s_hup,
    r_hup,
    s_hdn,
    r_hdn,
    s_mup,
    r_mup,
    s_mdn,
    r_mdn,
    s_rup,
    r_rup,
    s_rdn,
    r_rdn,
    s_gt,
    r_gt,
    s_ge,
    r_ge,
):
    n_edge, n_tile, edges, frames, rows, width, slots = dims
    band = rows * width
    halo = RADIUS * width
    me = lax.axis_index("edge")
    tile = lax.axis_index("tile")
    up, down = tile - 1, tile + 1
    has_up, has_down = tile > 0, tile < n_tile - 1

    loads = [
        pltpu.make_async_copy(feat_h, feat, l_in.at[0]),
        pltpu.make_async_copy(hidden_h, hext.at[:, pl.ds(width, band)], l_in.at[1]),
    ]
    fills = []
    for a in range(3):
        for b in range(3):
            at = pl.ds((a * 3 + b) * 128, 128)
            first, second = pl.ds(0, 128), pl.ds(128, 128)
            pairs = (
                (gate_w.at[a, b, first], wh.at[at]),
                (gate_w.at[a, b, second], wm.at[at, pl.ds(0, 256)]),
                (cand_w.at[a, b, second], wm.at[at, pl.ds(256, 128)]),
                (cand_w.at[a, b, first], wr.at[at]),
            )
            for source, target in pairs:
                fills.append(pltpu.make_async_copy(source, target, l_w.at[len(fills)]))
    for load in loads + fills:
        load.start()

    barrier = pltpu.get_barrier_semaphore()
    for rel in range(1, n_edge):
        pl.semaphore_signal(
            barrier, inc=1, device_id=((me + rel) % n_edge, tile), device_id_type=MESH
        )
    for rel in range(1, n_tile):
        pl.semaphore_signal(
            barrier, inc=1, device_id=(me, (tile + rel) % n_tile), device_id_type=MESH
        )
    pl.semaphore_wait(barrier, n_edge + n_tile - 2)

    def remote(src, dst, send_sem, recv_sem, edge_id, tile_id):
        return pltpu.make_async_remote_copy(
            src_ref=src,
            dst_ref=dst,
            send_sem=send_sem,
            recv_sem=recv_sem,
            device_id=(edge_id, tile_id),
            device_id_type=MESH,
        )

    def meta_copy(rel):
        return remote(
            meta_in, meta_all.at[me], s_meta.at[rel], r_meta.at[rel], (me + rel) % n_edge, tile
        )

    for rel in range(1, n_edge):
        meta_copy(rel).start()

    def hid_up(e):
        return remote(
            hidden_h.at[e, pl.ds(0, width)], hext.at[e, pl.ds(width + band, width)],
            s_hup.at[e], r_hup.at[e], me, up,
        )

    def hid_dn(e):
        return remote(
            hidden_h.at[e, pl.ds(band - width, width)], hext.at[e, pl.ds(0, width)],
            s_hdn.at[e], r_hdn.at[e], me, down,
        )

    def row_up(buf, s, r, e):
        return remote(
            buf.at[e, pl.ds(width, width)], buf.at[e, pl.ds(width + band, width)],
            s.at[e], r.at[e], me, up,
        )

    def row_dn(buf, s, r, e):
        return remote(
            buf.at[e, pl.ds(band, width)], buf.at[e, pl.ds(0, width)],
            s.at[e], r.at[e], me, down,
        )

    def txt_up(k):
        return remote(
            text.at[k, pl.ds(halo, halo)], text.at[k, pl.ds(halo + band, halo)],
            s_tup.at[k], r_tup.at[k], me, up,
        )

    def txt_dn(k):
        return remote(
            text.at[k, pl.ds(band, halo)], text.at[k, pl.ds(0, halo)],
            s_tdn.at[k], r_tdn.at[k], me, down,
        )

    def start_pair(make_up, make_dn):
        @pl.when(has_up)
        def _():
            make_up.start()

        @pl.when(has_down)
        def _():
            make_dn.start()

    def recv_pair(make_up, make_dn):
        @pl.when(has_down)
        def _():
            make_up.wait_recv()

        @pl.when(has_up)
        def _():
            make_dn.wait_recv()

    def sent_pair(make_up, make_dn):
        @pl.when(has_up)
        def _():
            make_up.wait_send()

        @pl.when(has_down)
        def _():
            make_dn.wait_send()

    def each(count, body):
        def step(i, carry):
            body(i)
            return carry

        lax.fori_loop(0, count, step, 0)

    each(edges, lambda e: start_pair(hid_up(e), hid_dn(e)))

    zero_row = jnp.zeros((width, 128), BF)
    zero_halo = jnp.zeros((halo, 128), BF)

    @pl.when(tile == 0)
    def _():
        def clear(e):
            for buf in (hext, mext, rext):
                buf[e, pl.ds(0, width)] = zero_row

        each(edges, clear)

        def clear_text(k):
            text[k, pl.ds(0, halo)] = zero_halo

        each(n_edge * slots, clear_text)

    @pl.when(tile == n_tile - 1)
    def _():
        def clear(e):
            for buf in (hext, mext, rext):
                buf[e, pl.ds(width + band, width)] = zero_row

        each(edges, clear)

        def clear_text(k):
            text[k, pl.ds(halo + band, halo)] = zero_halo

        each(n_edge * slots, clear_text)

    if (rows + 2 * RADIUS) % 2:

        def clear_pad(k):
            text[k, pl.ds(band + 2 * halo, width)] = zero_row

        each(n_edge * slots, clear_pad)

    meta_all[me] = meta_in[...]
    for rel in range(1, n_edge):
        remote(
            meta_in, meta_all.at[(me - rel + n_edge) % n_edge], s_meta.at[rel], r_meta.at[rel],
            (me + rel) % n_edge, tile,
        ).wait_recv()
    loads[0].wait()
    local = pltpu.make_async_copy(meta_all, meta_s, l_meta)
    local.start()
    local.wait()

    def asked(peer):
        picks = [jnp.int32(0)] * slots
        rank = jnp.int32(0)
        for k in range(edges):
            hit = (meta_s[peer, 0, k] == me).astype(jnp.int32)
            goal = meta_s[peer, 0, 8 + k]
            for s in range(slots):
                picks[s] = jnp.where((hit == 1) & (rank == s), goal, picks[s])
            rank = rank + hit
        return picks

    def feat_copy(rel, s):
        return remote(
            send.at[(rel - 1) * slots + s],
            text.at[rel * slots + s, pl.ds(halo, band)],
            s_feat.at[rel * slots + s],
            r_feat.at[rel * slots + s],
            (me - rel + n_edge) % n_edge,
            tile,
        )

    asks = [asked((me - rel + n_edge) % n_edge) for rel in range(n_edge)]
    for s in range(slots):
        for rel in range(1, n_edge):
            send[(rel - 1) * slots + s] = feat[asks[rel][s]]
        for rel in range(1, n_edge):
            feat_copy(rel, s).start()
    for s in range(slots):
        text[s, pl.ds(halo, band)] = feat[asks[0][s]]
    for s in range(slots):
        start_pair(txt_up(s), txt_dn(s))

    spot = iota((2 * width, 64), 0)
    rank = ((spot + 97) & 63) - 32
    second = ((spot + 97) & 127) >> 6
    names = iota((2 * width, 64), 1)
    lookup = jnp.concatenate(
        [corr_in[...].astype(F32), jnp.zeros((64 - WINDOW * WINDOW, 128), F32)], axis=0
    ).astype(BF)
    for par in range(2):
        for g in range(4):
            down_by = 2 * g - par + second
            fits = (rank >= -RADIUS) & (rank <= RADIUS) & (down_by >= 0) & (down_by < WINDOW)
            pick = (names == down_by * WINDOW + rank + RADIUS) & fits
            corr_w[par, pl.ds(g * 2 * width, 2 * width)] = nn(
                pick.astype(F32).astype(BF), lookup
            ).astype(BF)

    place12 = iota((32, 64), 0)
    which = place12 >> 4
    within = place12 & 15
    name12 = iota((32, 64), 1)
    pick_j = (within < 12) & (name12 == which * 12 + within)
    padded_jac = jnp.concatenate(
        [jac_in[...].astype(F32), jnp.zeros((40, 128), F32)], axis=0
    ).astype(BF)
    conf_wide = conf_in[...].astype(F32)
    tall = iota((32, 128), 0)
    conf_rows = jnp.where(
        tall < 16,
        jnp.broadcast_to(conf_wide[0:1], (32, 128)),
        jnp.broadcast_to(conf_wide[1:2], (32, 128)),
    )
    head_w = jnp.concatenate(
        [
            nn(pick_j.astype(F32).astype(BF), padded_jac),
            jnp.where((tall & 15) < 12, conf_rows, 0.0),
        ],
        axis=0,
    ).astype(BF)

    col = iota((band + 2 * width, 128), 0) & (width - 1)

    group = 2 if edges % 2 == 0 else 1

    def shifted(buf, first):
        parts = []
        for q in range(group):
            value = buf[first + q]
            wide = value.astype(F32)
            left = jnp.where(col == 0, 0.0, pltpu.roll(wide, 1, 0)).astype(BF)
            right = jnp.where(
                col == width - 1, 0.0, pltpu.roll(wide, band + 2 * width - 1, 0)
            ).astype(BF)
            x3[q, :, 0:128] = left
            x3[q, :, 128:256] = value
            x3[q, :, 256:384] = right
        for q in range(group):
            parts.append(
                jnp.concatenate(
                    [x3[q, a * width : a * width + band] for a in range(3)], axis=1
                )
            )
        return jnp.concatenate(parts, axis=0)

    def grouped(body):
        each(edges // group, lambda i: body(i * group))

    flip_row, flip_col = iota((2 * width, 2 * width), 0), iota((2 * width, 2 * width), 1)
    flip = (
        ((flip_row >= width) == (flip_col >= width))
        & ((flip_row & (width - 1)) + (flip_col & (width - 1)) == width - 1)
    ).astype(F32).astype(BF)

    def flipped(value):
        count = value.shape[0]
        return nn(flip[0:count, 0:count], value).astype(BF)

    def state_part(e):
        for q in range(group):
            recv_pair(hid_up(e + q), hid_dn(e + q))
        for q in range(group):
            source = feat[meta_s[me, 0, 16 + e + q]]
            for first in range(0, rows, 2):
                last = min(rows, first + 2) * width
                sref[e + q, pl.ds(first * width, last - first * width)] = flipped(
                    source[first * width : last]
                )
        value = nn(shifted(hext, e), wh[...])
        for q in range(group):
            gpre[e + q] = value[q * band : (q + 1) * band]

    loads[1].wait()
    for fill in fills:
        fill.wait()
    grouped(state_part)

    for s in range(slots):
        for rel in range(1, n_edge):
            feat_copy(rel, s).wait_recv()
            start_pair(txt_up(rel * slots + s), txt_dn(rel * slots + s))
    each(n_edge * slots, lambda k: recv_pair(txt_up(k), txt_dn(k)))

    lane = iota((width, 128), 1)
    place = (width - 1 - iota((width, 128), 0)) + ((lane + 97) & 63) - 32
    inside = (place >= 0) & (place < width)
    scale = 128.0 ** (-0.5)

    def slot_of(e):
        mine = meta_s[me, 0, e]
        rank = jnp.int32(0)
        for k in range(edges):
            rank = rank + jnp.where((meta_s[me, 0, k] == mine) & (k < e), 1, 0)
        return ((mine - me + n_edge) % n_edge) * slots + jnp.minimum(rank, slots - 1)

    def motion_of(e):
        k = slot_of(e)
        source = sref[e]
        target = text[k]
        for first in range(0, rows, 2):
            count = min(2, rows - first)
            table = nt(
                source[first * width : (first + count) * width],
                target[first * width : (first + 8) * width],
            )
            values = []
            for par in range(count):
                parts = []
                for g in range(4):
                    piece = table[par * width : (par + 1) * width, g * 128 : (g + 1) * 128]
                    moved = pltpu.roll(piece, 0, 1, stride=1, stride_axis=0)
                    parts.append(jnp.where(inside, moved * scale, 0.0).astype(BF))
                value = nn(jnp.concatenate(parts, axis=1), corr_w[par])
                values.append(jnp.maximum(value, 0.0).astype(BF))
            mext[e, pl.ds((first + 1) * width, count * width)] = flipped(
                jnp.concatenate(values, axis=0)
            )

    def motion(e):
        for q in range(group):
            motion_of(e + q)
        for q in range(group):
            start_pair(
                row_up(mext, s_mup, r_mup, e + q), row_dn(mext, s_mdn, r_mdn, e + q)
            )

    grouped(motion)

    def gates(e):
        for q in range(group):
            recv_pair(
                row_up(mext, s_mup, r_mup, e + q), row_dn(mext, s_mdn, r_mdn, e + q)
            )
        both = nn(shifted(mext, e), wm[...])
        for q in range(group):
            part = both[q * band : (q + 1) * band]
            cpre[e + q] = part[:, 256:384]
            gate = jax.nn.sigmoid(gpre[e + q] + part[:, 0:256])
            upd[e + q] = gate[:, 0:128]
            state = hext[e + q, pl.ds(width, band)].astype(F32)
            rext[e + q, pl.ds(width, band)] = (gate[:, 128:256] * state).astype(BF)
        for q in range(group):
            start_pair(
                row_up(rext, s_rup, r_rup, e + q), row_dn(rext, s_rdn, r_rdn, e + q)
            )

    grouped(gates)

    def finish(e):
        for q in range(group):
            recv_pair(
                row_up(rext, s_rup, r_rup, e + q), row_dn(rext, s_rdn, r_rdn, e + q)
            )
        mixed = nn(shifted(rext, e), wr[...])
        for q in range(group):
            candidate = jnp.tanh(cpre[e + q] + mixed[q * band : (q + 1) * band])
            update = upd[e + q]
            state = hext[e + q, pl.ds(width, band)]
            fresh = ((1.0 - update) * state.astype(F32) + update * candidate).astype(BF)
            used = (e + q < meta_s[me, 0, 24]).astype(F32)
            live = jnp.full((band, 128), used) > 0.5
            held[e + q] = jnp.where(live, fresh, state)
            heads = nt(head_w, fresh)
            jac = heads[0:32]
            weighted = jac * jax.nn.softplus(heads[32:64])
            at16 = pl.ds(pl.multiple_of((e + q) * 16, 16), 16)
            jall[at16] = jnp.concatenate([jac[0:16], jac[16:32]], axis=1).astype(BF)
            wall[at16] = jnp.concatenate([weighted[0:16], weighted[16:32]], axis=1).astype(BF)

    grouped(finish)
    store = pltpu.make_async_copy(held, out_hidden, l_out)
    store.start()

    same = (iota((128, 128), 0) >> 4) == (iota((128, 128), 1) >> 4)
    square = jnp.where(same, nt(wall[...], jall[...]), 0.0)
    blocks = square[0:16]
    for e in range(1, edges):
        blocks = blocks + square[e * 16 : (e + 1) * 16]
    alive = (iota((16, 128), 1) >> 4) < meta_s[me, 0, 24]
    gpart[...] = jnp.where(alive, blocks * (1.0 / (MAPH * width)), 0.0)

    def tile_copy(rel):
        return remote(
            gpart, gtile.at[tile], s_gt.at[rel], r_gt.at[rel], me, (tile + rel) % n_tile
        )

    for rel in range(1, n_tile):
        tile_copy(rel).start()
    gtile[tile] = gpart[...]
    for rel in range(1, n_tile):
        remote(
            gpart, gtile.at[(tile - rel + n_tile) % n_tile], s_gt.at[rel], r_gt.at[rel],
            me, (tile + rel) % n_tile,
        ).wait_recv()
    total = gtile[0]
    for k in range(1, n_tile):
        total = total + gtile[k]
    gsum[...] = total

    def edge_copy(rel):
        return remote(gsum, gall.at[me], s_ge.at[rel], r_ge.at[rel], (me + rel) % n_edge, tile)

    for rel in range(1, n_edge):
        edge_copy(rel).start()
    gall[me] = total
    for rel in range(1, n_edge):
        remote(
            gsum, gall.at[(me - rel + n_edge) % n_edge], s_ge.at[rel], r_ge.at[rel],
            (me + rel) % n_edge, tile,
        ).wait_recv()

    store.wait()
    for rel in range(1, n_edge):
        meta_copy(rel).wait_send()
        edge_copy(rel).wait_send()
        for s in range(slots):
            feat_copy(rel, s).wait_send()
    for rel in range(1, n_tile):
        tile_copy(rel).wait_send()
    each(n_edge * slots, lambda k: sent_pair(txt_up(k), txt_dn(k)))

    def sent(e):
        sent_pair(hid_up(e), hid_dn(e))
        sent_pair(row_up(mext, s_mup, r_mup, e), row_dn(mext, s_mdn, r_mdn, e))
        sent_pair(row_up(rext, s_rup, r_rup, e), row_dn(rext, s_rdn, r_rdn, e))

    each(edges, sent)


def halves(value):
    high = value.astype(BF)
    return high, (value - high.astype(F32)).astype(BF)


def assemble(dims, meta_s, gall, hidden_h, out_hidden, out_cam, out_diag, held, sem):
    n_edge, n_tile, edges, frames, rows, width, slots = dims
    fetch = pltpu.make_async_copy(hidden_h, held, sem.at[0])
    fetch.start()
    me = lax.axis_index("edge")
    tile = lax.axis_index("tile")
    cam_rows, cam_cols = out_cam.shape
    row_id = iota((cam_rows, 128), 0) + tile * cam_rows
    col_id = iota((cam_cols, 128), 0) + me * cam_cols
    same = (iota((128, 128), 0) >> 4) == (iota((128, 128), 1) >> 4)
    lane = iota((1, 128), 1)
    inner = lane & 15
    digit = jnp.where(inner < 6, inner, inner - 6)
    lefts, lows, rights = [], [], []
    for j in range(n_edge):
        spots = jnp.full((1, 128), -1, jnp.int32)
        for e in range(edges):
            source = (j * frames + meta_s[j, 0, 16 + e]) * 6
            target = (meta_s[j, 0, e] * frames + meta_s[j, 0, 8 + e]) * 6
            here = jnp.where(inner < 6, source, target) + digit
            spots = jnp.where(((lane >> 4) == e) & (inner < 12), here, spots)
        mine = (col_id == spots).astype(F32)
        left = jnp.concatenate([(row_id == spots).astype(F32), mine], axis=0).astype(BF)
        stack = jnp.where(same, jnp.concatenate([gall[j]] * 8, axis=0), 0.0)
        picked = nn(
            jnp.concatenate([left, left], axis=1), jnp.concatenate(halves(stack), axis=0)
        )
        high, low = halves(picked)
        lefts.append(high)
        lows.append(low)
        rights.append(mine.astype(BF))
    placed = nt(jnp.concatenate(lefts + lows, axis=1), jnp.concatenate(rights + rights, axis=1))
    fetch.wait()
    store = pltpu.make_async_copy(held, out_hidden, sem.at[1])
    store.start()
    cam = placed[0:cam_rows]
    row_frame = sixth(iota((cam_rows, cam_cols), 0) + tile * cam_rows)
    col_frame = sixth(iota((cam_rows, cam_cols), 1) + me * cam_cols)
    out_cam[...] = jnp.where(row_frame == col_frame, 0.0, cam)
    own = placed[cam_rows:]
    own_row = sixth(iota((cam_cols, cam_cols), 0))
    own_col = sixth(iota((cam_cols, cam_cols), 1))
    own = jnp.where(own_row == own_col, own, 0.0)
    wide_row = iota((cam_cols, 128), 0)
    wide_lane = iota((cam_cols, 128), 1)
    row_in = wide_row.astype(F32) - 6.0 * sixth(wide_row)
    lane_of = sixth(wide_lane)
    lane_in = wide_lane.astype(F32) - 6.0 * lane_of
    gather = (row_in == lane_in).astype(F32).astype(BF)
    high, low = halves(own)
    spread = jnp.where(row_in == lane_of, nn(high, gather) + nn(low, gather), 0.0)
    fold = (
        sixth(iota((frames, cam_cols), 1)) == iota((frames, cam_cols), 0).astype(F32)
    ).astype(F32).astype(BF)
    high, low = halves(spread)
    out_diag[...] = (nn(fold, high) + nn(fold, low))[:, 0:36]
    store.wait()


def per_device(
    features,
    hidden_state,
    edge_source,
    edge_owner,
    edge_target,
    edge_counts,
    corr_weight,
    gate_weight,
    candidate_weight,
    jacobian_weight,
    confidence_weight,
):
    n_edge, n_tile = lax.axis_size("edge"), lax.axis_size("tile")
    edges = hidden_state.shape[0]
    frames, rows, width, chan = features.shape
    slots = max(2, (2 * edges + n_edge - 1) // n_edge)
    band = rows * width
    owners = edge_owner[:, 0]

    fields = ((owners, 0), (edge_target, 8), (edge_source, 16), (edge_counts, 24))
    meta = jnp.zeros((1, 128), jnp.int32)
    for field, at in fields:
        meta = meta + jnp.pad(field, (at, 128 - at - field.shape[0]))[None, :]
    dims = (n_edge, n_tile, edges, frames, rows, width, slots)
    total_slots = n_edge * slots
    text_rows = rows + 2 * RADIUS
    text_rows = text_rows + text_rows % 2
    ext = band + 2 * width
    dma = pltpu.SemaphoreType.DMA
    vmem = pl.BlockSpec(memory_space=pltpu.VMEM)
    hbm = pl.BlockSpec(memory_space=pl.ANY)
    state, gall, meta_all = pl.pallas_call(
        functools.partial(kernel, dims),
        out_shape=(
            jax.ShapeDtypeStruct((edges, band, chan), BF),
            jax.ShapeDtypeStruct((n_edge, 16, 128), F32),
            jax.ShapeDtypeStruct((n_edge, 1, 128), jnp.int32),
        ),
        in_specs=[vmem, hbm, hbm, vmem, hbm, hbm, vmem, vmem],
        out_specs=(hbm, vmem, vmem),
        scratch_shapes=[
            pltpu.VMEM((frames, band, chan), BF),
            pltpu.VMEM((edges, band, chan), BF),
            dma,
            pltpu.VMEM((2, 8 * width, chan), BF),
            pltpu.VMEM((edges * 16, 2 * band), BF),
            pltpu.VMEM((edges * 16, 2 * band), BF),
            pltpu.SMEM((n_edge, 1, 128), jnp.int32),
            pltpu.VMEM(((n_edge - 1) * slots, band, chan), BF),
            pltpu.VMEM((total_slots, text_rows * width, chan), BF),
            pltpu.VMEM((edges, band, chan), BF),
            pltpu.VMEM((edges, ext, chan), BF),
            pltpu.VMEM((edges, ext, chan), BF),
            pltpu.VMEM((edges, ext, chan), BF),
            pltpu.VMEM((2, ext, 3 * chan), BF),
            pltpu.VMEM((9 * chan, 2 * chan), BF),
            pltpu.VMEM((9 * chan, 3 * chan), BF),
            pltpu.VMEM((9 * chan, chan), BF),
            pltpu.VMEM((edges, band, 2 * chan), F32),
            pltpu.VMEM((edges, band, chan), F32),
            pltpu.VMEM((edges, band, chan), F32),
            pltpu.VMEM((16, 128), F32),
            pltpu.VMEM((n_tile, 16, 128), F32),
            pltpu.VMEM((16, 128), F32),
            dma((2,)),
            dma((36,)),
            dma((n_edge,)),
            dma((n_edge,)),
            dma,
            dma((total_slots,)),
            dma((total_slots,)),
        ]
        + [dma((total_slots,))] * 4
        + [dma((edges,))] * 12
        + [dma((n_tile,)), dma((n_tile,)), dma((n_edge,)), dma((n_edge,))],
        compiler_params=pltpu.CompilerParams(
            collective_id=0, has_side_effects=True, vmem_limit_bytes=56 * 1024 * 1024
        ),
    )(
        meta,
        features.reshape(frames, band, chan),
        hidden_state.reshape(edges, band, chan),
        corr_weight,
        gate_weight,
        candidate_weight,
        jacobian_weight.T,
        confidence_weight.T,
    )
    hidden_next, cam, diag = pl.pallas_call(
        functools.partial(assemble, dims),
        out_shape=(
            jax.ShapeDtypeStruct((edges, band, chan), BF),
            jax.ShapeDtypeStruct((frames * n_edge * 6 // n_tile, frames * 6), F32),
            jax.ShapeDtypeStruct((frames, 36), F32),
        ),
        in_specs=[pl.BlockSpec(memory_space=pltpu.SMEM), vmem, hbm],
        out_specs=(hbm, vmem, vmem),
        scratch_shapes=[pltpu.VMEM((edges, band, chan), BF), dma((2,))],
    )(meta_all, gall, state)
    return hidden_next.reshape(hidden_state.shape), cam, diag


def solution(mesh):
    placed = (
        P("edge", "tile", None, None),
        P("edge", "tile", None, None),
        P("edge"),
        P("edge", None),
        P("edge"),
        P("edge"),
        P(),
        P(),
        P(),
        P(),
        P(),
    )
    return jax.shard_map(
        per_device,
        mesh=mesh,
        in_specs=placed,
        out_specs=(P("edge", "tile", None, None), P("tile", "edge"), P("edge", None)),
        check_vma=False,
    )
```

profile of v0, /device:TPU:0, one launch (start us, length us, event | category | flops | bytes accessed | tf_op | source)
XLA Modules:
  0.0 65.3 jit_solution(6009093044678636430)
XLA Ops:
  1.3 1.3 %add_bitcast_fusion.meta_in = s32[1,128]{1,0:T(1,128)} fusion(s32[1]{0:T(128)S(6)} %copy.14, s32[8]{0:T(128)} %param.13, s32[8]{0:T(128)} %param.15, s32[8]{0:T(128)} %bitcast.12), kind=kLoop, calls=%fused_computation | loop fusion | flops 384 | bytes 612 | tf_op jit(solution)/shard_map/add | solution.py:645
  2.6 59.1 %shard_map.130 = (bf16[8,384,128]{2,1,0:T(8,128)(2,1)}, f32[4,16,128]{2,1,0:T(8,128)}, s32[4,1,128]{2,1,0:T(1,128)}) custom-call(s32[1,128]{1,0:T(1,128)} %add_bitcast_fusion.meta_in, bf16[24,384,128]{2,1,0:T(8,128)(2,1)} %bitcast.8, bf16[8,384,128]{2,1,0:T(8,128)(2,1)} %bitcast.9, bf16[49,128]{1,0:T(8,128)(2,1)} %corr_in.1, ...), custom_call_target="tpu_custom_call" | custom-call | tf_op jit(solution)/shard_map/pallas_call | solution.py:654
  61.7 3.5 %shard_map.131 = (bf16[8,384,128]{2,1,0:T(8,128)(2,1)}, f32[72,144]{1,0:T(8,128)}, f32[24,36]{1,0:T(8,128)}) custom-call(s32[4,1,128]{2,1,0:T(1,128)} %get-tuple-element.9.meta_s, f32[4,16,128]{2,1,0:T(8,128)} %get-tuple-element.10.gall, bf16[8,384,128]{2,1,0:T(8,128)(2,1)} %get-tuple-element.11.hidden_h), custom_call_target="tpu_custom_call" | custom-call | tf_op jit(solution)/shard_map/pallas_call | solution.py:711
where the time goes:
time: 65.6 us; the launch traced here: 65.3 us
  Pallas kernels  62.7 us (96%)
  between operations  1.29 us (2%)
  other arithmetic  1.28 us (2%)
    pallas_call x1, Pallas kernels, per_device(): pl.pallas_call(functools.partial(kernel, dims), out_shape=(jax.ShapeDtype...  59.1 us
    pallas_call x1, Pallas kernels, per_device(): pl.pallas_call(functools.partial(assemble, dims), out_shape=(jax.ShapeDty...  3.55 us

commit v1 on v0

v1 whole, which is shorter than its diff:
```python
import functools
import types

import jax
import jax.numpy as jnp
from jax import lax
from jax.experimental import pallas as pl
from jax.experimental.pallas import tpu as pltpu
from jax.sharding import PartitionSpec as P

MAPH = 48
WINDOW = 7
RADIUS = WINDOW // 2
NEAR = 2
FAR = RADIUS + NEAR
OWNER, TARGET, SOURCE, COUNT, PLACE, GROUP, REL, ASKS = 0, 8, 16, 24, 32, 40, 48, 64
MESH = pl.DeviceIdType.MESH
BF = jnp.bfloat16
F32 = jnp.float32


def nt(a, b):
    return lax.dot_general(a, b, (((1,), (1,)), ((), ())), preferred_element_type=F32)


def nn(a, b):
    return lax.dot_general(a, b, (((1,), (0,)), ((), ())), preferred_element_type=F32)


def iota(shape, dim):
    return lax.broadcasted_iota(jnp.int32, shape, dim)


def sixth(index):
    return jnp.floor((index.astype(F32) + 0.5) * (1.0 / 6.0))


def one_hot(cond):
    return cond.astype(F32).astype(BF)


def each(count, body):
    def step(i, carry):
        body(i)
        return carry

    lax.fori_loop(0, count, step, 0)


def reach(halo, rows):
    return [min(rows, halo - d * rows) for d in range((halo + rows - 1) // rows)]


def kernel(dims, names, *refs):
    n_edge, n_tile, edges, frames, rows, width, slots = dims
    r = types.SimpleNamespace(**dict(zip(names, refs)))
    band = rows * width
    per = edges // slots
    me = lax.axis_index("edge")
    tile = lax.axis_index("tile")
    texts = [getattr(r, f"text{s}") for s in range(slots)]

    loads = [
        pltpu.make_async_copy(r.feat_h, r.feat, r.l_in.at[0]),
        pltpu.make_async_copy(
            r.hidden_h, r.hext.at[:, pl.ds(NEAR * width, band)], r.l_in.at[1]
        ),
    ]
    fills = []
    for a in range(3):
        for b in range(3):
            at = pl.ds((a * 3 + b) * 128, 128)
            first, second = pl.ds(0, 128), pl.ds(128, 128)
            pairs = (
                (r.gate_w.at[a, b, first], r.wh.at[at]),
                (r.gate_w.at[a, b, second], r.wm.at[at, pl.ds(0, 256)]),
                (r.cand_w.at[a, b, second], r.wm.at[at, pl.ds(256, 128)]),
                (r.cand_w.at[a, b, first], r.wr.at[at]),
            )
            for source, target in pairs:
                fills.append(pltpu.make_async_copy(source, target, r.l_w.at[len(fills)]))
    for load in loads + fills:
        load.start()

    barrier = pltpu.get_barrier_semaphore()
    for rel in range(1, n_edge):
        pl.semaphore_signal(
            barrier, inc=1, device_id=((me + rel) % n_edge, tile), device_id_type=MESH
        )
    for rel in range(1, n_tile):
        pl.semaphore_signal(
            barrier, inc=1, device_id=(me, (tile + rel) % n_tile), device_id_type=MESH
        )

    owner = [r.own_s[0, OWNER + e] for e in range(edges)]
    rel_of = [(owner[e] - me + n_edge) % n_edge for e in range(edges)]
    rank, group = [], []
    for e in range(edges):
        before = jnp.int32(0)
        for k in range(e):
            before = before + (owner[k] == owner[e]).astype(jnp.int32)
        rank.append(jnp.minimum(before, slots - 1))
        group.append(jnp.where(rel_of[e] == 0, 0, rank[e] + 1))
    lane = iota((1, 128), 1)
    row = jnp.where(lane == COUNT, r.own_s[0, COUNT], 0)
    for e in range(edges):
        spot = jnp.int32(0)
        for k in range(edges):
            if k < e:
                spot = spot + (group[k] <= group[e]).astype(jnp.int32)
            elif k > e:
                spot = spot + (group[k] < group[e]).astype(jnp.int32)
        goal = r.own_s[0, TARGET + e]
        fields = (
            (OWNER, owner[e]),
            (TARGET, goal),
            (SOURCE, r.own_s[0, SOURCE + e]),
            (PLACE, jnp.int32(e)),
            (GROUP, group[e]),
            (REL, rel_of[e]),
        )
        for base, value in fields:
            row = jnp.where(lane == base + spot, value, row)
        row = jnp.where(lane == ASKS + rel_of[e] * slots + rank[e], goal, row)
    r.row_v[...] = row
    mine = pltpu.make_async_copy(r.row_v, r.row_s, r.l_row)
    mine.start()
    mine.wait()

    pl.semaphore_wait(barrier, n_edge + n_tile - 2)

    def remote(src, dst, send_sem, recv_sem, edge_id, tile_id):
        return pltpu.make_async_remote_copy(
            src_ref=src,
            dst_ref=dst,
            send_sem=send_sem,
            recv_sem=recv_sem,
            device_id=(edge_id, tile_id),
            device_id_type=MESH,
        )

    def meta_copy(rel):
        return remote(
            r.row_v, r.meta_all.at[me], r.s_meta.at[rel], r.r_meta.at[rel],
            (me + rel) % n_edge, tile,
        )

    for rel in range(1, n_edge):
        meta_copy(rel).start()

    class Halo:
        def __init__(self, halo, buf, source, sems):
            self.halo, self.buf, self.source, self.sems = halo, buf, source, sems
            self.counts = reach(halo, rows)

        def copies(self, e):
            for d, count in enumerate(self.counts):
                far, lines = d + 1, count * width
                s_up, r_up, s_dn, r_dn = self.sems
                up = remote(
                    self.source(e, 0, lines),
                    self.buf.at[e, pl.ds((self.halo + far * rows) * width, lines)],
                    s_up.at[d, e], r_up.at[d, e], me, tile - far,
                )
                dn = remote(
                    self.source(e, band - lines, lines),
                    self.buf.at[e, pl.ds((self.halo - d * rows - count) * width, lines)],
                    s_dn.at[d, e], r_dn.at[d, e], me, tile + far,
                )
                yield tile >= far, tile + far < n_tile, up, dn

        def start(self, e):
            for above, below, up, dn in self.copies(e):
                pl.when(above)(up.start)
                pl.when(below)(dn.start)

        def received(self, e):
            for above, below, up, dn in self.copies(e):
                pl.when(below)(up.wait_recv)
                pl.when(above)(dn.wait_recv)

        def sent(self, e):
            for above, below, up, dn in self.copies(e):
                pl.when(above)(up.wait_send)
                pl.when(below)(dn.wait_send)

        def clear(self):
            for d, count in enumerate(self.counts):
                far, lines = d + 1, count * width
                zero = jnp.zeros((lines, 128), BF)
                top = (self.halo - d * rows - count) * width
                low = (self.halo + far * rows) * width

                @pl.when(tile < far)
                def _():
                    def clear_top(e):
                        self.buf[e, pl.ds(top, lines)] = zero

                    each(edges, clear_top)

                @pl.when(tile + far >= n_tile)
                def _():
                    def clear_low(e):
                        self.buf[e, pl.ds(low, lines)] = zero

                    each(edges, clear_low)

            used = (rows + 2 * self.halo) * width
            spare = self.buf.shape[1] - used
            if spare:

                def clear_pad(e):
                    self.buf[e, pl.ds(used, spare)] = jnp.zeros((spare, 128), BF)

                each(edges, clear_pad)

    def inner(buf, halo):
        return lambda e, at, lines: buf.at[e, pl.ds(halo * width + at, lines)]

    hid = Halo(
        NEAR, r.hext, lambda e, at, lines: r.hidden_h.at[e, pl.ds(at, lines)],
        (r.s_hup, r.r_hup, r.s_hdn, r.r_hdn),
    )
    src = Halo(NEAR, r.sext, inner(r.sext, NEAR), (r.s_sup, r.r_sup, r.s_sdn, r.r_sdn))
    txt = Halo(FAR, r.text, inner(r.text, FAR), (r.s_tup, r.r_tup, r.s_tdn, r.r_tdn))

    each(edges, hid.start)
    r.meta_all[me] = r.row_v[...]
    for rel in range(1, n_edge):
        remote(
            r.row_v, r.meta_all.at[(me - rel + n_edge) % n_edge], r.s_meta.at[rel],
            r.r_meta.at[rel], (me + rel) % n_edge, tile,
        ).wait_recv()
    local = pltpu.make_async_copy(r.meta_all, r.meta_s, r.l_meta)
    local.start()
    loads[0].wait()
    local.wait()

    def feat_copy(rel, s):
        return remote(
            r.send.at[(rel - 1) * slots + s], texts[s].at[rel - 1],
            r.s_feat.at[rel, s], r.r_feat.at[rel, s], (me - rel + n_edge) % n_edge, tile,
        )

    for s in range(slots):
        for rel in range(1, n_edge):
            peer = (me - rel + n_edge) % n_edge
            r.send[(rel - 1) * slots + s] = r.feat[r.meta_s[peer, 0, ASKS + rel * slots + s]]
        for rel in range(1, n_edge):
            feat_copy(rel, s).start()

    def take_source(e):
        r.sext[e, pl.ds(NEAR * width, band)] = r.feat[r.row_s[0, SOURCE + e]]
        src.start(e)

    each(edges, take_source)
    for halo in (hid, src, txt):
        halo.clear()

    far_off = iota((width, 128), 0) - (iota((width, 128), 1) & (width - 1))
    scaled = jnp.where((far_off >= -RADIUS) & (far_off <= RADIUS), 128.0 ** (-0.5), 0.0)
    deep = 8 * width
    column = iota((deep, 128), 0) & 7
    r.fold[...] = one_hot(
        (iota((deep, 128), 1) & 63) == (((8 - column) & 7) << 3) + iota((deep, 128), 0) // width
    )
    spot = iota((128, 64), 0)
    turn = (spot & 63) >> 3
    across = jnp.where(turn > 4, 8 - turn, -turn)
    along = (spot & 7) - (spot >> 6)
    fits = (turn != 4) & (along >= 0) & (along < WINDOW)
    pick = (iota((128, 64), 1) == along * WINDOW + across + RADIUS) & fits
    lookup = jnp.concatenate(
        [r.corr_in[...].astype(F32), jnp.zeros((64 - WINDOW * WINDOW, 128), F32)], axis=0
    ).astype(BF)
    r.corr_w[...] = nn(one_hot(pick), lookup).astype(BF)

    place12 = iota((32, 64), 0)
    which = place12 >> 4
    within = place12 & 15
    name12 = iota((32, 64), 1)
    pick_j = (within < 12) & (name12 == which * 12 + within)
    padded_jac = jnp.concatenate(
        [r.jac_in[...].astype(F32), jnp.zeros((40, 128), F32)], axis=0
    ).astype(BF)
    conf_wide = r.conf_in[...].astype(F32)
    tall = iota((32, 128), 0)
    conf_rows = jnp.where(
        tall < 16,
        jnp.broadcast_to(conf_wide[0:1], (32, 128)),
        jnp.broadcast_to(conf_wide[1:2], (32, 128)),
    )
    r.head_w[...] = jnp.concatenate(
        [nn(one_hot(pick_j), padded_jac), jnp.where((tall & 15) < 12, conf_rows, 0.0)], axis=0
    ).astype(BF)

    def shifted(values, out_rows):
        parts = []
        for q, value in enumerate(values):
            lines = value.shape[0]
            column = iota((lines, 128), 0) & (width - 1)
            wide = value.astype(F32)
            left = jnp.where(column == 0, 0.0, pltpu.roll(wide, 1, 0)).astype(BF)
            right = jnp.where(column == width - 1, 0.0, pltpu.roll(wide, lines - 1, 0)).astype(BF)
            r.x3[q, 0:lines, 0:128] = left
            r.x3[q, 0:lines, 128:256] = value
            r.x3[q, 0:lines, 256:384] = right
        size = out_rows * width
        for q in range(len(values)):
            parts.append(
                jnp.concatenate(
                    [r.x3[q, a * width : a * width + size] for a in range(3)], axis=1
                )
            )
        return jnp.concatenate(parts, axis=0)

    wide_band = (rows + 2) * width

    def state_part(p):
        values = []
        for q in range(per):
            e = p * per + q
            values.append(r.hext[r.row_s[0, PLACE + e]])
        value = nn(shifted(values, rows + 2), r.wh[...])
        for q in range(per):
            r.gpre[p * per + q] = value[q * wide_band : (q + 1) * wide_band]

    loads[1].wait()
    for fill in fills:
        fill.wait()
    each(edges, hid.received)
    each(slots, state_part)
    each(edges, src.received)

    half = (iota((2 * width, 128), 1) >> 6) == iota((2 * width, 128), 0) // width
    pairs_of = (rows + 2 * NEAR + 1) // 2

    def motion_of(e, q):
        for k in range(pairs_of):
            at = 2 * k * width
            table = nt(r.sext[e, pl.ds(at, 2 * width)], r.text[e, pl.ds(at, deep)])
            lines = []
            for par in range(2):
                lines.append(
                    jnp.concatenate(
                        [
                            table[par * width : (par + 1) * width, g * 128 : (g + 1) * 128] * scaled
                            for g in range(deep // 128)
                        ],
                        axis=1,
                    )
                )
            banded = jnp.concatenate(lines, axis=0).astype(BF)
            folded = pltpu.roll(nn(banded, r.fold[...]), 0, 1, stride=8, stride_axis=0)
            value = nn(jnp.where(half, folded, 0.0).astype(BF), r.corr_w[...])
            count = min(2, rows + 2 * NEAR - 2 * k) * width
            r.mext[q, pl.ds(at, count)] = jnp.maximum(value, 0.0).astype(BF)[0:count]

    def update(p):
        for q in range(per):
            txt.received(p * per + q)
        for q in range(per):
            motion_of(p * per + q, q)
        both = nn(shifted([r.mext[q] for q in range(per)], rows + 2), r.wm[...])
        for q in range(per):
            e = p * per + q
            part = both[q * wide_band : (q + 1) * wide_band]
            r.cpre[q] = part[width : width + band, 256:384]
            before = r.gpre[e] + part[:, 0:256]
            r.upd[q] = 0.5 * jnp.tanh(0.5 * before[width : width + band, 0:128]) + 0.5
            reset = 0.5 * jnp.tanh(0.5 * before[:, 128:256]) + 0.5
            state = r.hext[r.row_s[0, PLACE + e], pl.ds(width, wide_band)].astype(F32)
            r.rext[q] = (reset * state).astype(BF)
        mixed = nn(shifted([r.rext[q] for q in range(per)], rows), r.wr[...])
        for q in range(per):
            e = p * per + q
            candidate = jnp.tanh(r.cpre[q] + mixed[q * band : (q + 1) * band])
            gate = r.upd[q]
            place = r.row_s[0, PLACE + e]
            state = r.hext[place, pl.ds(NEAR * width, band)]
            fresh = ((1.0 - gate) * state.astype(F32) + gate * candidate).astype(BF)
            used = (place < r.row_s[0, COUNT]).astype(F32)
            live = jnp.full((band, 128), used) > 0.5
            r.held[e] = jnp.where(live, fresh, state)
            heads = nt(r.head_w[...], fresh)
            jac = heads[0:32]
            weighted = jac * jax.nn.softplus(heads[32:64])
            at16 = pl.ds(pl.multiple_of(e * 16, 16), 16)
            r.jall[at16] = jnp.concatenate([jac[0:16], jac[16:32]], axis=1).astype(BF)
            r.wall[at16] = jnp.concatenate([weighted[0:16], weighted[16:32]], axis=1).astype(BF)

    def take_target(e, upto):
        value = r.feat[r.row_s[0, TARGET + e]]
        at = jnp.maximum(r.row_s[0, REL + e] - 1, 0)
        for s in range(upto + 1):
            value = jnp.where(r.row_s[0, GROUP + e] == s + 1, texts[s][at], value)
        r.text[e, pl.ds(FAR * width, band)] = value
        txt.start(e)

    def stage(p):
        for s in range(slots):

            @pl.when(p == s)
            def _():
                for rel in range(1, n_edge):
                    feat_copy(rel, s).wait_recv()
                for q in range(per):
                    take_target(s * per + q, s)

        pl.when(p > 0)(lambda: update(p - 1))

    each(slots + 1, stage)
    store = pltpu.make_async_copy(r.held, r.out_hidden, r.l_out)
    store.start()

    same = (iota((128, 128), 0) >> 4) == (iota((128, 128), 1) >> 4)
    square = jnp.where(same, nt(r.wall[...], r.jall[...]), 0.0)
    blocks = square[0:16]
    for e in range(1, edges):
        blocks = blocks + square[e * 16 : (e + 1) * 16]
    blocks = blocks * (1.0 / (MAPH * width))
    of = iota((16, 128), 1) >> 4
    for e in range(edges):
        used = (r.row_s[0, PLACE + e] < r.row_s[0, COUNT]).astype(jnp.int32)
        blocks = jnp.where((of == e) & (jnp.full((16, 128), used) == 0), 0.0, blocks)
    r.gpart[...] = blocks

    def tile_copy(rel):
        return remote(
            r.gpart, r.gtile.at[tile], r.s_gt.at[rel], r.r_gt.at[rel], me, (tile + rel) % n_tile
        )

    for rel in range(1, n_tile):
        tile_copy(rel).start()
    r.gtile[tile] = r.gpart[...]
    for rel in range(1, n_tile):
        remote(
            r.gpart, r.gtile.at[(tile - rel + n_tile) % n_tile], r.s_gt.at[rel], r.r_gt.at[rel],
            me, (tile + rel) % n_tile,
        ).wait_recv()
    total = r.gtile[0]
    for k in range(1, n_tile):
        total = total + r.gtile[k]
    r.gsum[...] = total

    def edge_copy(rel):
        return remote(
            r.gsum, r.gall.at[me], r.s_ge.at[rel], r.r_ge.at[rel], (me + rel) % n_edge, tile
        )

    for rel in range(1, n_edge):
        edge_copy(rel).start()
    r.gall[me] = total
    for rel in range(1, n_edge):
        remote(
            r.gsum, r.gall.at[(me - rel + n_edge) % n_edge], r.s_ge.at[rel], r.r_ge.at[rel],
            (me + rel) % n_edge, tile,
        ).wait_recv()

    store.wait()
    for rel in range(1, n_edge):
        meta_copy(rel).wait_send()
        edge_copy(rel).wait_send()
        for s in range(slots):
            feat_copy(rel, s).wait_send()
    for rel in range(1, n_tile):
        tile_copy(rel).wait_send()
    for halo in (hid, src, txt):
        each(edges, halo.sent)


def halves(value):
    high = value.astype(BF)
    return high, (value - high.astype(F32)).astype(BF)


def assemble(dims, meta_s, gall, hidden_h, out_hidden, out_cam, out_diag, held, sem):
    n_edge, n_tile, edges, frames, rows, width, slots = dims
    me = lax.axis_index("edge")
    tile = lax.axis_index("tile")
    fetch = pltpu.make_async_copy(hidden_h, held, sem.at[edges])
    fetch.start()
    cam_rows, cam_cols = out_cam.shape
    row_id = iota((cam_rows, 128), 0) + tile * cam_rows
    col_id = iota((cam_cols, 128), 0) + me * cam_cols
    same = (iota((128, 128), 0) >> 4) == (iota((128, 128), 1) >> 4)
    lane = iota((1, 128), 1)
    inner = lane & 15
    digit = jnp.where(inner < 6, inner, inner - 6)
    lefts, lows, rights = [], [], []
    for j in range(n_edge):
        spots = jnp.full((1, 128), -1, jnp.int32)
        for e in range(edges):
            source = (j * frames + meta_s[j, 0, SOURCE + e]) * 6
            target = (meta_s[j, 0, OWNER + e] * frames + meta_s[j, 0, TARGET + e]) * 6
            here = jnp.where(inner < 6, source, target) + digit
            spots = jnp.where(((lane >> 4) == e) & (inner < 12), here, spots)
        mine = (col_id == spots).astype(F32)
        left = jnp.concatenate([(row_id == spots).astype(F32), mine], axis=0).astype(BF)
        stack = jnp.where(same, jnp.concatenate([gall[j]] * 8, axis=0), 0.0)
        picked = nn(
            jnp.concatenate([left, left], axis=1), jnp.concatenate(halves(stack), axis=0)
        )
        high, low = halves(picked)
        lefts.append(high)
        lows.append(low)
        rights.append(mine.astype(BF))
    placed = nt(jnp.concatenate(lefts + lows, axis=1), jnp.concatenate(rights + rights, axis=1))
    fetch.wait()
    stores = [
        pltpu.make_async_copy(held.at[e], out_hidden.at[meta_s[me, 0, PLACE + e]], sem.at[e])
        for e in range(edges)
    ]
    for store in stores:
        store.start()
    cam = placed[0:cam_rows]
    row_frame = sixth(iota((cam_rows, cam_cols), 0) + tile * cam_rows)
    col_frame = sixth(iota((cam_rows, cam_cols), 1) + me * cam_cols)
    out_cam[...] = jnp.where(row_frame == col_frame, 0.0, cam)
    own = placed[cam_rows:]
    own_row = sixth(iota((cam_cols, cam_cols), 0))
    own_col = sixth(iota((cam_cols, cam_cols), 1))
    own = jnp.where(own_row == own_col, own, 0.0)
    wide_row = iota((cam_cols, 128), 0)
    wide_lane = iota((cam_cols, 128), 1)
    row_in = wide_row.astype(F32) - 6.0 * sixth(wide_row)
    lane_of = sixth(wide_lane)
    lane_in = wide_lane.astype(F32) - 6.0 * lane_of
    gather = one_hot(row_in == lane_in)
    high, low = halves(own)
    spread = jnp.where(row_in == lane_of, nn(high, gather) + nn(low, gather), 0.0)
    fold = one_hot(
        sixth(iota((frames, cam_cols), 1)) == iota((frames, cam_cols), 0).astype(F32)
    )
    high, low = halves(spread)
    out_diag[...] = (nn(fold, high) + nn(fold, low))[:, 0:36]
    for store in stores:
        store.wait()


def per_device(
    features,
    hidden_state,
    edge_source,
    edge_owner,
    edge_target,
    edge_counts,
    corr_weight,
    gate_weight,
    candidate_weight,
    jacobian_weight,
    confidence_weight,
):
    n_edge, n_tile = lax.axis_size("edge"), lax.axis_size("tile")
    edges = hidden_state.shape[0]
    frames, rows, width, chan = features.shape
    slots = max(2, (2 * edges + n_edge - 1) // n_edge)
    assert edges % slots == 0 and edges <= 8 and ASKS + n_edge * slots <= 128
    per = edges // slots
    band = rows * width

    fields = (
        (edge_owner[:, 0], OWNER), (edge_target, TARGET), (edge_source, SOURCE), (edge_counts, COUNT),
    )
    meta = jnp.zeros((1, 128), jnp.int32)
    for field, at in fields:
        meta = meta + jnp.pad(field, (at, 128 - at - field.shape[0]))[None, :]
    dims = (n_edge, n_tile, edges, frames, rows, width, slots)
    even = (rows + 2 * NEAR + 1) // 2 * 2
    dma = pltpu.SemaphoreType.DMA
    vmem = pl.BlockSpec(memory_space=pltpu.VMEM)
    smem = pl.BlockSpec(memory_space=pltpu.SMEM)
    hbm = pl.BlockSpec(memory_space=pl.ANY)

    inputs = (
        ("own_s", meta, smem),
        ("feat_h", features.reshape(frames, band, chan), hbm),
        ("hidden_h", hidden_state.reshape(edges, band, chan), hbm),
        ("corr_in", corr_weight, vmem),
        ("gate_w", gate_weight, hbm),
        ("cand_w", candidate_weight, hbm),
        ("jac_in", jacobian_weight.T, vmem),
        ("conf_in", confidence_weight.T, vmem),
    )
    outputs = (
        ("out_hidden", (edges, band, chan), BF, hbm),
        ("gall", (n_edge, 16, 128), F32, vmem),
        ("meta_all", (n_edge, 1, 128), jnp.int32, vmem),
    )
    near, far = len(reach(NEAR, rows)), len(reach(FAR, rows))
    scratch = {
        "row_v": pltpu.VMEM((1, 128), jnp.int32),
        "row_s": pltpu.SMEM((1, 128), jnp.int32),
        "meta_s": pltpu.SMEM((n_edge, 1, 128), jnp.int32),
        "feat": pltpu.VMEM((frames, band, chan), BF),
        "held": pltpu.VMEM((edges, band, chan), BF),
        "send": pltpu.VMEM(((n_edge - 1) * slots, band, chan), BF),
        "text": pltpu.VMEM((edges, (even + 2 * RADIUS) * width, chan), BF),
        "sext": pltpu.VMEM((edges, even * width, chan), BF),
        "hext": pltpu.VMEM((edges, (rows + 2 * NEAR) * width, chan), BF),
        "mext": pltpu.VMEM((per, (rows + 2 * NEAR) * width, chan), BF),
        "rext": pltpu.VMEM((per, (rows + 2) * width, chan), BF),
        "x3": pltpu.VMEM((per, (rows + 2 * NEAR) * width, 3 * chan), BF),
        "wh": pltpu.VMEM((9 * chan, 2 * chan), BF),
        "wm": pltpu.VMEM((9 * chan, 3 * chan), BF),
        "wr": pltpu.VMEM((9 * chan, chan), BF),
        "fold": pltpu.VMEM((8 * width, 128), BF),
        "corr_w": pltpu.VMEM((128, chan), BF),
        "head_w": pltpu.VMEM((64, chan), BF),
        "gpre": pltpu.VMEM((edges, (rows + 2) * width, 2 * chan), F32),
        "cpre": pltpu.VMEM((per, band, chan), F32),
        "upd": pltpu.VMEM((per, band, chan), F32),
        "jall": pltpu.VMEM((128, 2 * band), BF),
        "wall": pltpu.VMEM((128, 2 * band), BF),
        "gpart": pltpu.VMEM((16, 128), F32),
        "gtile": pltpu.VMEM((n_tile, 16, 128), F32),
        "gsum": pltpu.VMEM((16, 128), F32),
        "l_in": dma((2,)),
        "l_w": dma((36,)),
        "l_row": dma,
        "l_meta": dma,
        "l_out": dma,
        "s_meta": dma((n_edge,)),
        "r_meta": dma((n_edge,)),
        "s_feat": dma((n_edge, slots)),
        "r_feat": dma((n_edge, slots)),
        "s_gt": dma((n_tile,)),
        "r_gt": dma((n_tile,)),
        "s_ge": dma((n_edge,)),
        "r_ge": dma((n_edge,)),
    }
    for s in range(slots):
        scratch[f"text{s}"] = pltpu.VMEM((n_edge - 1, band, chan), BF)
    for key, count in (("h", near), ("s", near), ("t", far)):
        for name in (f"s_{key}up", f"r_{key}up", f"s_{key}dn", f"r_{key}dn"):
            scratch[name] = dma((count, edges))
    names = [i[0] for i in inputs] + [o[0] for o in outputs] + list(scratch)
    state, gall, meta_all = pl.pallas_call(
        functools.partial(kernel, dims, names),
        out_shape=tuple(jax.ShapeDtypeStruct(shape, kind) for _, shape, kind, _ in outputs),
        in_specs=[spec for _, _, spec in inputs],
        out_specs=tuple(spec for _, _, _, spec in outputs),
        scratch_shapes=list(scratch.values()),
        compiler_params=pltpu.CompilerParams(
            collective_id=0, has_side_effects=True, vmem_limit_bytes=56 * 1024 * 1024
        ),
    )(*[value for _, value, _ in inputs])
    hidden_next, cam, diag = pl.pallas_call(
        functools.partial(assemble, dims),
        out_shape=(
            jax.ShapeDtypeStruct((edges, band, chan), BF),
            jax.ShapeDtypeStruct((frames * n_edge * 6 // n_tile, frames * 6), F32),
            jax.ShapeDtypeStruct((frames, 36), F32),
        ),
        in_specs=[smem, vmem, hbm],
        out_specs=(hbm, vmem, vmem),
        scratch_shapes=[pltpu.VMEM((edges, band, chan), BF), dma((edges + 1,))],
    )(meta_all, gall, state)
    return hidden_next.reshape(hidden_state.shape), cam, diag


def solution(mesh):
    placed = (
        P("edge", "tile", None, None),
        P("edge", "tile", None, None),
        P("edge"),
        P("edge", None),
        P("edge"),
        P("edge"),
        P(),
        P(),
        P(),
        P(),
        P(),
    )
    return jax.shard_map(
        per_device,
        mesh=mesh,
        in_specs=placed,
        out_specs=(P("edge", "tile", None, None), P("tile", "edge"), P("edge", None)),
        check_vma=False,
    )
```

time: 65.6 us -> 61.7 us (0.941)
  Pallas kernels: 62.7 us -> 58.9 us
    pallas_call x1, Pallas kernels: 59.1 us -> 55.3 us  [per_device(): pl.pallas_call(functools.partial(kernel, dims, names), out_shape=tuple((j...]
where the time goes in v1:
time: 61.7 us; the launch traced here: 61.4 us
  Pallas kernels  58.9 us (95%)
  between operations  1.29 us (2%)
  other arithmetic  1.28 us (2%)
    pallas_call x1, Pallas kernels, per_device(): pl.pallas_call(functools.partial(kernel, dims, names), out_shape=tuple((j...  55.3 us
    pallas_call x1, Pallas kernels, per_device(): pl.pallas_call(functools.partial(assemble, dims), out_shape=(jax.ShapeDty...  3.59 us
    add x1, other arithmetic, per_device(): meta = meta + jnp.pad(field, (at, 128 - at - field.shape[0]))[None, :]  1.28 us

profile of v1, /device:TPU:0, one launch (start us, length us, event | category | flops | bytes accessed | tf_op | source)
XLA Modules:
  0.0 61.4 jit_solution(2163611441611643380)
XLA Ops:
  1.3 1.3 %add_bitcast_fusion.refs_0_ = s32[1,128]{1,0:T(1,128)} fusion(s32[1]{0:T(128)S(6)} %copy.14, s32[8]{0:T(128)} %param.13, s32[8]{0:T(128)} %param.15, s32[8]{0:T(128)} %bitcast.12), kind=kLoop, calls=%fused_computation | loop fusion | flops 384 | bytes 612 | tf_op jit(solution)/shard_map/add | solution.py:567
  2.6 55.3 %shard_map.130 = (bf16[8,384,128]{2,1,0:T(8,128)(2,1)}, f32[4,16,128]{2,1,0:T(8,128)}, s32[4,1,128]{2,1,0:T(1,128)}) custom-call(s32[1,128]{1,0:T(1,128)} %add_bitcast_fusion.refs_0_, bf16[24,384,128]{2,1,0:T(8,128)(2,1)} %bitcast.8, bf16[8,384,128]{2,1,0:T(8,128)(2,1)} %bitcast.9, bf16[49,128]{1,0:T(8,128)(2,1)} %refs_3_.1, ...), custom_call_target="tpu_custom_call" | custom-call | tf_op jit(solution)/shard_map/pallas_call | solution.py:638
  57.8 3.6 %shard_map.131 = (bf16[8,384,128]{2,1,0:T(8,128)(2,1)}, f32[72,144]{1,0:T(8,128)}, f32[24,36]{1,0:T(8,128)}) custom-call(s32[4,1,128]{2,1,0:T(1,128)} %get-tuple-element.9.meta_s, f32[4,16,128]{2,1,0:T(8,128)} %get-tuple-element.10.gall, bf16[8,384,128]{2,1,0:T(8,128)(2,1)} %get-tuple-element.11.hidden_h), custom_call_target="tpu_custom_call" | custom-call | tf_op jit(solution)/shard_map/pallas_call | solution.py:648

commit v2 on v1

--- a/solution.py
+++ b/solution.py
@@ -73,9 +73,9 @@
             first, second = pl.ds(0, 128), pl.ds(128, 128)
             pairs = (
                 (r.gate_w.at[a, b, first], r.wh.at[at]),
-                (r.gate_w.at[a, b, second], r.wm.at[at, pl.ds(0, 256)]),
-                (r.cand_w.at[a, b, second], r.wm.at[at, pl.ds(256, 128)]),
-                (r.cand_w.at[a, b, first], r.wr.at[at]),
+                (r.gate_w.at[a, b, second], r.wm.at[at]),
+                (r.cand_w.at[a, b, first], r.wc.at[pl.ds(b * 128, 128), pl.ds(a * 128, 128)]),
+                (r.cand_w.at[a, b, second], r.wc.at[pl.ds(384 + b * 128, 128), pl.ds(a * 128, 128)]),
             )
             for source, target in pairs:
                 fills.append(pltpu.make_async_copy(source, target, r.l_w.at[len(fills)]))
@@ -257,19 +257,11 @@
     for halo in (hid, src, txt):
         halo.clear()
 
-    far_off = iota((width, 128), 0) - (iota((width, 128), 1) & (width - 1))
-    scaled = jnp.where((far_off >= -RADIUS) & (far_off <= RADIUS), 128.0 ** (-0.5), 0.0)
-    deep = 8 * width
-    column = iota((deep, 128), 0) & 7
-    r.fold[...] = one_hot(
-        (iota((deep, 128), 1) & 63) == (((8 - column) & 7) << 3) + iota((deep, 128), 0) // width
-    )
-    spot = iota((128, 64), 0)
-    turn = (spot & 63) >> 3
-    across = jnp.where(turn > 4, 8 - turn, -turn)
-    along = (spot & 7) - (spot >> 6)
-    fits = (turn != 4) & (along >= 0) & (along < WINDOW)
-    pick = (iota((128, 64), 1) == along * WINDOW + across + RADIUS) & fits
+    spot = (iota((128, 64), 0) + 4) & 127
+    along = ((spot >> 3) & 3) * 2 + (spot >> 6) - ((spot >> 5) & 1)
+    across = WINDOW - 1 - (spot & 7)
+    fits = (across >= 0) & (along >= 0) & (along < WINDOW)
+    pick = (iota((128, 64), 1) == along * WINDOW + across) & fits
     lookup = jnp.concatenate(
         [r.corr_in[...].astype(F32), jnp.zeros((64 - WINDOW * WINDOW, 128), F32)], axis=0
     ).astype(BF)
@@ -294,34 +286,32 @@
         [nn(one_hot(pick_j), padded_jac), jnp.where((tall & 15) < 12, conf_rows, 0.0)], axis=0
     ).astype(BF)
 
-    def shifted(values, out_rows):
-        parts = []
-        for q, value in enumerate(values):
-            lines = value.shape[0]
-            column = iota((lines, 128), 0) & (width - 1)
-            wide = value.astype(F32)
-            left = jnp.where(column == 0, 0.0, pltpu.roll(wide, 1, 0)).astype(BF)
-            right = jnp.where(column == width - 1, 0.0, pltpu.roll(wide, lines - 1, 0)).astype(BF)
-            r.x3[q, 0:lines, 0:128] = left
-            r.x3[q, 0:lines, 128:256] = value
-            r.x3[q, 0:lines, 256:384] = right
+    def spread(value, out):
+        lines = value.shape[0]
+        column = iota((lines, 128), 0) & (width - 1)
+        wide = value.astype(F32)
+        left = jnp.where(column == 0, 0.0, pltpu.roll(wide, 1, 0)).astype(BF)
+        right = jnp.where(column == width - 1, 0.0, pltpu.roll(wide, lines - 1, 0)).astype(BF)
+        out[0:lines, 0:128] = left
+        out[0:lines, 128:256] = value
+        out[0:lines, 256:384] = right
+
+    def windows(x3, out_rows):
         size = out_rows * width
-        for q in range(len(values)):
-            parts.append(
-                jnp.concatenate(
-                    [r.x3[q, a * width : a * width + size] for a in range(3)], axis=1
-                )
-            )
-        return jnp.concatenate(parts, axis=0)
+        return jnp.concatenate(
+            [
+                jnp.concatenate([x3[q, a * width : a * width + size] for a in range(3)], axis=1)
+                for q in range(per)
+            ],
+            axis=0,
+        )
 
     wide_band = (rows + 2) * width
 
     def state_part(p):
-        values = []
         for q in range(per):
-            e = p * per + q
-            values.append(r.hext[r.row_s[0, PLACE + e]])
-        value = nn(shifted(values, rows + 2), r.wh[...])
+            spread(r.hext[r.row_s[0, PLACE + p * per + q]], r.x3.at[q])
+        value = nn(windows(r.x3, rows + 2), r.wh[...])
         for q in range(per):
             r.gpre[p * per + q] = value[q * wide_band : (q + 1) * wide_band]
 
@@ -332,49 +322,84 @@
     each(slots, state_part)
     each(edges, src.received)
 
-    half = (iota((2 * width, 128), 1) >> 6) == iota((2 * width, 128), 0) // width
+    lane_w = (iota((width, 128), 1) + 4) & 127
+    col_w = iota((width, 128), 0) + RADIUS - (lane_w & 7)
+    in_map = (col_w >= 0) & (col_w < width) & ((lane_w & 7) < WINDOW)
+    scaled = [
+        jnp.where(in_map & (((lane_w >> 5) & 1) == par), 128.0 ** (-0.5), 0.0) for par in range(2)
+    ]
+    slot_w = (lane_w >> 3) & 3
     pairs_of = (rows + 2 * NEAR + 1) // 2
+    quads_of = r.text.shape[1] // (4 * width)
 
     def motion_of(e, q):
+        tables, starts = [], []
+        for m in range(quads_of):
+            first, last = max(0, 2 * m - 3), min(pairs_of - 1, 2 * m + 1)
+            starts.append(first)
+            tables.append(
+                nt(
+                    r.sext[e, pl.ds(2 * first * width, 2 * (last - first + 1) * width)],
+                    r.text[e, pl.ds(4 * m * width, 4 * width)],
+                )
+            )
+        lines = []
         for k in range(pairs_of):
-            at = 2 * k * width
-            table = nt(r.sext[e, pl.ds(at, 2 * width)], r.text[e, pl.ds(at, deep)])
-            lines = []
             for par in range(2):
-                lines.append(
-                    jnp.concatenate(
-                        [
-                            table[par * width : (par + 1) * width, g * 128 : (g + 1) * 128] * scaled
-                            for g in range(deep // 128)
-                        ],
-                        axis=1,
+                found = None
+                for g in range(4):
+                    m, h = divmod(k + g, 2)
+                    at = (2 * (k - starts[m]) + par) * width
+                    piece = tables[m][at : at + width, h * 128 : (h + 1) * 128]
+                    moved = pltpu.roll(
+                        piece, width + 8 * g + 32 * par, 1, stride=1, stride_axis=0
                     )
-                )
-            banded = jnp.concatenate(lines, axis=0).astype(BF)
-            folded = pltpu.roll(nn(banded, r.fold[...]), 0, 1, stride=8, stride_axis=0)
-            value = nn(jnp.where(half, folded, 0.0).astype(BF), r.corr_w[...])
-            count = min(2, rows + 2 * NEAR - 2 * k) * width
-            r.mext[q, pl.ds(at, count)] = jnp.maximum(value, 0.0).astype(BF)[0:count]
+                    found = moved if g == 0 else jnp.where(slot_w == g, moved, found)
+                lines.append((found * scaled[par]).astype(BF))
+        value = nn(jnp.concatenate(lines, axis=0), r.corr_w[...])
+        r.mext[q] = jnp.maximum(value, 0.0).astype(BF)
+
+    used_rows = (rows + 2 * NEAR) * width
 
     def update(p):
         for q in range(per):
             txt.received(p * per + q)
         for q in range(per):
             motion_of(p * per + q, q)
-        both = nn(shifted([r.mext[q] for q in range(per)], rows + 2), r.wm[...])
+        for q in range(per):
+            spread(r.mext[q, 0:used_rows], r.x3.at[q])
+        both = nn(windows(r.x3, rows + 2), r.wm[...])
         for q in range(per):
             e = p * per + q
-            part = both[q * wide_band : (q + 1) * wide_band]
-            r.cpre[q] = part[width : width + band, 256:384]
-            before = r.gpre[e] + part[:, 0:256]
+            before = r.gpre[e] + both[q * wide_band : (q + 1) * wide_band]
             r.upd[q] = 0.5 * jnp.tanh(0.5 * before[width : width + band, 0:128]) + 0.5
             reset = 0.5 * jnp.tanh(0.5 * before[:, 128:256]) + 0.5
             state = r.hext[r.row_s[0, PLACE + e], pl.ds(width, wide_band)].astype(F32)
-            r.rext[q] = (reset * state).astype(BF)
-        mixed = nn(shifted([r.rext[q] for q in range(per)], rows), r.wr[...])
+            spread((reset * state).astype(BF), r.x3r.at[q])
+
+        def inputs(first, count):
+            first, count = first * width, count * width
+            return jnp.concatenate(
+                [
+                    jnp.concatenate(
+                        [
+                            r.x3r[q, first : first + count],
+                            r.x3[q, width + first : width + first + count],
+                        ],
+                        axis=1,
+                    )
+                    for q in range(per)
+                ],
+                axis=0,
+            )
+
+        upper = nn(inputs(0, rows + 1), r.wc[:, 0:256])
+        lower = nn(inputs(2, rows), r.wc[:, 256:384])
         for q in range(per):
             e = p * per + q
-            candidate = jnp.tanh(r.cpre[q] + mixed[q * band : (q + 1) * band])
+            at = q * (rows + 1) * width
+            mixed = upper[at : at + band, 0:128] + upper[at + width : at + width + band, 128:256]
+            candidate = jnp.tanh(mixed + lower[q * band : (q + 1) * band])
             gate = r.upd[q]
             place = r.row_s[0, PLACE + e]
             state = r.hext[place, pl.ds(NEAR * width, band)]
@@ -389,12 +414,22 @@
             r.jall[at16] = jnp.concatenate([jac[0:16], jac[16:32]], axis=1).astype(BF)
             r.wall[at16] = jnp.concatenate([weighted[0:16], weighted[16:32]], axis=1).astype(BF)
 
+    flip_row, flip_col = iota((2 * width, 2 * width), 0), iota((2 * width, 2 * width), 1)
+    flip = one_hot(
+        (flip_row // width == flip_col // width)
+        & ((flip_row & (width - 1)) + (flip_col & (width - 1)) == width - 1)
+    )
+
     def take_target(e, upto):
         value = r.feat[r.row_s[0, TARGET + e]]
         at = jnp.maximum(r.row_s[0, REL + e] - 1, 0)
         for s in range(upto + 1):
             value = jnp.where(r.row_s[0, GROUP + e] == s + 1, texts[s][at], value)
-        r.text[e, pl.ds(FAR * width, band)] = value
+        for first in range(0, band, 2 * width):
+            count = min(2 * width, band - first)
+            r.text[e, pl.ds(FAR * width + first, count)] = nn(
+                flip[0:count, 0:count], value[first : first + count]
+            ).astype(BF)
         txt.start(e)
 
     def stage(p):
@@ -595,20 +630,18 @@
         "feat": pltpu.VMEM((frames, band, chan), BF),
         "held": pltpu.VMEM((edges, band, chan), BF),
         "send": pltpu.VMEM(((n_edge - 1) * slots, band, chan), BF),
-        "text": pltpu.VMEM((edges, (even + 2 * RADIUS) * width, chan), BF),
+        "text": pltpu.VMEM((edges, (even + 2 * RADIUS + 3) // 4 * 4 * width, chan), BF),
         "sext": pltpu.VMEM((edges, even * width, chan), BF),
         "hext": pltpu.VMEM((edges, (rows + 2 * NEAR) * width, chan), BF),
-        "mext": pltpu.VMEM((per, (rows + 2 * NEAR) * width, chan), BF),
-        "rext": pltpu.VMEM((per, (rows + 2) * width, chan), BF),
+        "mext": pltpu.VMEM((per, even * width, chan), BF),
         "x3": pltpu.VMEM((per, (rows + 2 * NEAR) * width, 3 * chan), BF),
+        "x3r": pltpu.VMEM((per, (rows + 2) * width, 3 * chan), BF),
         "wh": pltpu.VMEM((9 * chan, 2 * chan), BF),
-        "wm": pltpu.VMEM((9 * chan, 3 * chan), BF),
-        "wr": pltpu.VMEM((9 * chan, chan), BF),
-        "fold": pltpu.VMEM((8 * width, 128), BF),
+        "wm": pltpu.VMEM((9 * chan, 2 * chan), BF),
+        "wc": pltpu.VMEM((6 * chan, 3 * chan), BF),
         "corr_w": pltpu.VMEM((128, chan), BF),
         "head_w": pltpu.VMEM((64, chan), BF),
         "gpre": pltpu.VMEM((edges, (rows + 2) * width, 2 * chan), F32),
-        "cpre": pltpu.VMEM((per, band, chan), F32),
         "upd": pltpu.VMEM((per, band, chan), F32),
         "jall": pltpu.VMEM((128, 2 * band), BF),
         "wall": pltpu.VMEM((128, 2 * band), BF),

time: 61.7 us -> 54.2 us (0.88)
  Pallas kernels: 58.9 us -> 51.3 us
    pallas_call x1, Pallas kernels: 55.3 us -> 47.7 us  [per_device(): pl.pallas_call(functools.partial(kernel, dims, names), out_shape=tuple((j...]
where the time goes in v2:
time: 54.2 us; the launch traced here: 53.9 us
  Pallas kernels  51.3 us (95%)
  between operations  1.29 us (2%)
  other arithmetic  1.28 us (2%)
    pallas_call x1, Pallas kernels, per_device(): pl.pallas_call(functools.partial(kernel, dims, names), out_shape=tuple((j...  47.7 us
    pallas_call x1, Pallas kernels, per_device(): pl.pallas_call(functools.partial(assemble, dims), out_shape=(jax.ShapeDty...  3.59 us
    add x1, other arithmetic, per_device(): meta = meta + jnp.pad(field, (at, 128 - at - field.shape[0]))[None, :]  1.28 us

profile of v2, /device:TPU:0, one launch (start us, length us, event | category | flops | bytes accessed | tf_op | source)
XLA Modules:
  0.0 53.9 jit_solution(16529998144732101250)
XLA Ops:
  1.3 1.3 %add_bitcast_fusion.refs_0_ = s32[1,128]{1,0:T(1,128)} fusion(s32[1]{0:T(128)S(6)} %copy.14, s32[8]{0:T(128)} %param.13, s32[8]{0:T(128)} %param.15, s32[8]{0:T(128)} %bitcast.12), kind=kLoop, calls=%fused_computation | loop fusion | flops 384 | bytes 612 | tf_op jit(solution)/shard_map/add | solution.py:602
  2.6 47.7 %shard_map.130 = (bf16[8,384,128]{2,1,0:T(8,128)(2,1)}, f32[4,16,128]{2,1,0:T(8,128)}, s32[4,1,128]{2,1,0:T(1,128)}) custom-call(s32[1,128]{1,0:T(1,128)} %add_bitcast_fusion.refs_0_, bf16[24,384,128]{2,1,0:T(8,128)(2,1)} %bitcast.8, bf16[8,384,128]{2,1,0:T(8,128)(2,1)} %bitcast.9, bf16[49,128]{1,0:T(8,128)(2,1)} %refs_3_.1, ...), custom_call_target="tpu_custom_call" | custom-call | tf_op jit(solution)/shard_map/pallas_call | solution.py:671
  50.3 3.6 %shard_map.131 = (bf16[8,384,128]{2,1,0:T(8,128)(2,1)}, f32[72,144]{1,0:T(8,128)}, f32[24,36]{1,0:T(8,128)}) custom-call(s32[4,1,128]{2,1,0:T(1,128)} %get-tuple-element.9.meta_s, f32[4,16,128]{2,1,0:T(8,128)} %get-tuple-element.10.gall, bf16[8,384,128]{2,1,0:T(8,128)(2,1)} %get-tuple-element.11.hidden_h), custom_call_target="tpu_custom_call" | custom-call | tf_op jit(solution)/shard_map/pallas_call | solution.py:681

commit v3 on v2

--- a/solution.py
+++ b/solution.py
@@ -74,8 +74,8 @@
             pairs = (
                 (r.gate_w.at[a, b, first], r.wh.at[at]),
                 (r.gate_w.at[a, b, second], r.wm.at[at]),
-                (r.cand_w.at[a, b, first], r.wc.at[pl.ds(b * 128, 128), pl.ds(a * 128, 128)]),
-                (r.cand_w.at[a, b, second], r.wc.at[pl.ds(384 + b * 128, 128), pl.ds(a * 128, 128)]),
+                (r.cand_w.at[a, b, first], r.wc.at[pl.ds(a * 128, 128), pl.ds(b * 128, 128)]),
+                (r.cand_w.at[a, b, second], r.wc.at[pl.ds(384 + a * 128, 128), pl.ds(b * 128, 128)]),
             )
             for source, target in pairs:
                 fills.append(pltpu.make_async_copy(source, target, r.l_w.at[len(fills)]))
@@ -286,34 +286,30 @@
         [nn(one_hot(pick_j), padded_jac), jnp.where((tall & 15) < 12, conf_rows, 0.0)], axis=0
     ).astype(BF)
 
+    def nudge(wide, by):
+        lines = wide.shape[0]
+        column = iota((lines, 128), 0) & (width - 1)
+        edge = 0 if by == 1 else width - 1
+        return jnp.where(column == edge, 0.0, pltpu.roll(wide, by % lines, 0))
+
     def spread(value, out):
         lines = value.shape[0]
-        column = iota((lines, 128), 0) & (width - 1)
         wide = value.astype(F32)
-        left = jnp.where(column == 0, 0.0, pltpu.roll(wide, 1, 0)).astype(BF)
-        right = jnp.where(column == width - 1, 0.0, pltpu.roll(wide, lines - 1, 0)).astype(BF)
-        out[0:lines, 0:128] = left
-        out[0:lines, 128:256] = value
-        out[0:lines, 256:384] = right
-
-    def windows(x3, out_rows):
+        out[0:lines, 0:128] = nudge(wide, 1).astype(BF)
+        out[0:lines, 128:256] = value.astype(BF)
+        out[0:lines, 256:384] = nudge(wide, -1).astype(BF)
+
+    def windows(x3, q, out_rows):
         size = out_rows * width
-        return jnp.concatenate(
-            [
-                jnp.concatenate([x3[q, a * width : a * width + size] for a in range(3)], axis=1)
-                for q in range(per)
-            ],
-            axis=0,
-        )
+        return jnp.concatenate([x3[q, a * width : a * width + size] for a in range(3)], axis=1)
 
     wide_band = (rows + 2) * width
 
     def state_part(p):
         for q in range(per):
-            spread(r.hext[r.row_s[0, PLACE + p * per + q]], r.x3.at[q])
-        value = nn(windows(r.x3, rows + 2), r.wh[...])
-        for q in range(per):
-            r.gpre[p * per + q] = value[q * wide_band : (q + 1) * wide_band]
+            e = p * per + q
+            spread(r.hext[r.row_s[0, PLACE + e]], r.x3.at[q])
+            r.gpre[e] = nn(windows(r.x3, q, rows + 2), r.wh[...])
 
     loads[1].wait()
     for fill in fills:
@@ -331,6 +327,7 @@
     slot_w = (lane_w >> 3) & 3
     pairs_of = (rows + 2 * NEAR + 1) // 2
     quads_of = r.text.shape[1] // (4 * width)
+    used_rows = (rows + 2 * NEAR) * width
 
     def motion_of(e, q):
         tables, starts = [], []
@@ -357,49 +354,35 @@
                     found = moved if g == 0 else jnp.where(slot_w == g, moved, found)
                 lines.append((found * scaled[par]).astype(BF))
         value = nn(jnp.concatenate(lines, axis=0), r.corr_w[...])
-        r.mext[q] = jnp.maximum(value, 0.0).astype(BF)
-
-    used_rows = (rows + 2 * NEAR) * width
+        spread(jnp.maximum(value[0:used_rows], 0.0), r.x3.at[q])
 
     def update(p):
         for q in range(per):
             txt.received(p * per + q)
-        for q in range(per):
             motion_of(p * per + q, q)
         for q in range(per):
-            spread(r.mext[q, 0:used_rows], r.x3.at[q])
-        both = nn(windows(r.x3, rows + 2), r.wm[...])
-        for q in range(per):
             e = p * per + q
-            before = r.gpre[e] + both[q * wide_band : (q + 1) * wide_band]
+            before = r.gpre[e] + nn(windows(r.x3, q, rows + 2), r.wm[...])
             r.upd[q] = 0.5 * jnp.tanh(0.5 * before[width : width + band, 0:128]) + 0.5
             reset = 0.5 * jnp.tanh(0.5 * before[:, 128:256]) + 0.5
             state = r.hext[r.row_s[0, PLACE + e], pl.ds(width, wide_band)].astype(F32)
-            spread((reset * state).astype(BF), r.x3r.at[q])
-
-        def inputs(first, count):
-            first, count = first * width, count * width
-            return jnp.concatenate(
-                [
-                    jnp.concatenate(
-                        [
-                            r.x3r[q, first : first + count],
-                            r.x3[q, width + first : width + first + count],
-                        ],
-                        axis=1,
-                    )
-                    for q in range(per)
-                ],
-                axis=0,
-            )
-
-        upper = nn(inputs(0, rows + 1), r.wc[:, 0:256])
-        lower = nn(inputs(2, rows), r.wc[:, 256:384])
+            r.rext[q] = (reset * state).astype(BF)
         for q in range(per):
             e = p * per + q
-            at = q * (rows + 1) * width
-            mixed = upper[at : at + band, 0:128] + upper[at + width : at + width + band, 128:256]
-            candidate = jnp.tanh(mixed + lower[q * band : (q + 1) * band])
+            part = nn(
+                jnp.concatenate(
+                    [r.rext[q, a * width : a * width + band] for a in range(3)]
+                    + [
+                        r.x3[q, (a + 1) * width : (a + 1) * width + band, 128:256]
+                        for a in range(3)
+                    ],
+                    axis=1,
+                ),
+                r.wc[...],
+            )
+            candidate = jnp.tanh(
+                nudge(part[:, 0:128], 1) + part[:, 128:256] + nudge(part[:, 256:384], -1)
+            )
             gate = r.upd[q]
             place = r.row_s[0, PLACE + e]
             state = r.hext[place, pl.ds(NEAR * width, band)]
@@ -633,9 +616,8 @@
         "text": pltpu.VMEM((edges, (even + 2 * RADIUS + 3) // 4 * 4 * width, chan), BF),
         "sext": pltpu.VMEM((edges, even * width, chan), BF),
         "hext": pltpu.VMEM((edges, (rows + 2 * NEAR) * width, chan), BF),
-        "mext": pltpu.VMEM((per, even * width, chan), BF),
+        "rext": pltpu.VMEM((per, (rows + 2) * width, chan), BF),
         "x3": pltpu.VMEM((per, (rows + 2 * NEAR) * width, 3 * chan), BF),
-        "x3r": pltpu.VMEM((per, (rows + 2) * width, 3 * chan), BF),
         "wh": pltpu.VMEM((9 * chan, 2 * chan), BF),
         "wm": pltpu.VMEM((9 * chan, 2 * chan), BF),
         "wc": pltpu.VMEM((6 * chan, 3 * chan), BF),

time: 54.2 us -> 51.6 us (0.952)
  Pallas kernels: 51.3 us -> 48.7 us
    pallas_call x1, Pallas kernels: 47.7 us -> 45.1 us  [per_device(): pl.pallas_call(functools.partial(kernel, dims, names), out_shape=tuple((j...]
where the time goes in v3:
time: 51.6 us; the launch traced here: 51.3 us
  Pallas kernels  48.7 us (94%)
  between operations  1.29 us (2%)
  other arithmetic  1.28 us (2%)
    pallas_call x1, Pallas kernels, per_device(): pl.pallas_call(functools.partial(kernel, dims, names), out_shape=tuple((j...  45.1 us
    pallas_call x1, Pallas kernels, per_device(): pl.pallas_call(functools.partial(assemble, dims), out_shape=(jax.ShapeDty...  3.59 us
    add x1, other arithmetic, per_device(): meta = meta + jnp.pad(field, (at, 128 - at - field.shape[0]))[None, :]  1.28 us

profile of v3, /device:TPU:0, one launch (start us, length us, event | category | flops | bytes accessed | tf_op | source)
XLA Modules:
  0.0 51.3 jit_solution(6174145212559423049)
XLA Ops:
  1.3 1.3 %add_bitcast_fusion.refs_0_ = s32[1,128]{1,0:T(1,128)} fusion(s32[1]{0:T(128)S(6)} %copy.14, s32[8]{0:T(128)} %param.13, s32[8]{0:T(128)} %param.15, s32[8]{0:T(128)} %bitcast.12), kind=kLoop, calls=%fused_computation | loop fusion | flops 384 | bytes 612 | tf_op jit(solution)/shard_map/add | solution.py:585
  2.6 45.1 %shard_map.130 = (bf16[8,384,128]{2,1,0:T(8,128)(2,1)}, f32[4,16,128]{2,1,0:T(8,128)}, s32[4,1,128]{2,1,0:T(1,128)}) custom-call(s32[1,128]{1,0:T(1,128)} %add_bitcast_fusion.refs_0_, bf16[24,384,128]{2,1,0:T(8,128)(2,1)} %bitcast.8, bf16[8,384,128]{2,1,0:T(8,128)(2,1)} %bitcast.9, bf16[49,128]{1,0:T(8,128)(2,1)} %refs_3_.1, ...), custom_call_target="tpu_custom_call" | custom-call | tf_op jit(solution)/shard_map/pallas_call | solution.py:653
  47.7 3.6 %shard_map.131 = (bf16[8,384,128]{2,1,0:T(8,128)(2,1)}, f32[72,144]{1,0:T(8,128)}, f32[24,36]{1,0:T(8,128)}) custom-call(s32[4,1,128]{2,1,0:T(1,128)} %get-tuple-element.9.meta_s, f32[4,16,128]{2,1,0:T(8,128)} %get-tuple-element.10.gall, bf16[8,384,128]{2,1,0:T(8,128)(2,1)} %get-tuple-element.11.hidden_h), custom_call_target="tpu_custom_call" | custom-call | tf_op jit(solution)/shard_map/pallas_call | solution.py:663

commit v4 on v3

--- a/solution.py
+++ b/solution.py
@@ -13,7 +13,7 @@
 RADIUS = WINDOW // 2
 NEAR = 2
 FAR = RADIUS + NEAR
-OWNER, TARGET, SOURCE, COUNT, PLACE, GROUP, REL, ASKS = 0, 8, 16, 24, 32, 40, 48, 64
+OWNER, TARGET, SOURCE, PLACE, GROUP, REL, ASKS = 0, 8, 16, 32, 40, 48, 64
 MESH = pl.DeviceIdType.MESH
 BF = jnp.bfloat16
 F32 = jnp.float32
@@ -60,11 +60,20 @@
     tile = lax.axis_index("tile")
     texts = [getattr(r, f"text{s}") for s in range(slots)]
 
+    ints = [
+        pltpu.make_async_copy(r.owner_h, r.owner_s, r.l_ints.at[0]),
+        pltpu.make_async_copy(r.target_h, r.target_s, r.l_ints.at[1]),
+        pltpu.make_async_copy(r.source_h, r.source_s, r.l_ints.at[2]),
+        pltpu.make_async_copy(r.count_h, r.count_s, r.l_ints.at[3]),
+    ]
     loads = [
         pltpu.make_async_copy(r.feat_h, r.feat, r.l_in.at[0]),
         pltpu.make_async_copy(
             r.hidden_h, r.hext.at[:, pl.ds(NEAR * width, band)], r.l_in.at[1]
         ),
+        pltpu.make_async_copy(r.corr_h, r.corr_in, r.l_in.at[2]),
+        pltpu.make_async_copy(r.jac_h, r.jac_in, r.l_in.at[3]),
+        pltpu.make_async_copy(r.conf_h, r.conf_in, r.l_in.at[4]),
     ]
     fills = []
     for a in range(3):
@@ -79,7 +88,7 @@
             )
             for source, target in pairs:
                 fills.append(pltpu.make_async_copy(source, target, r.l_w.at[len(fills)]))
-    for load in loads + fills:
+    for load in ints + loads + fills:
         load.start()
 
     barrier = pltpu.get_barrier_semaphore()
@@ -92,7 +101,9 @@
             barrier, inc=1, device_id=(me, (tile + rel) % n_tile), device_id_type=MESH
         )
 
-    owner = [r.own_s[0, OWNER + e] for e in range(edges)]
+    for load in ints:
+        load.wait()
+    owner = [r.owner_s[e] for e in range(edges)]
     rel_of = [(owner[e] - me + n_edge) % n_edge for e in range(edges)]
     rank, group = [], []
     for e in range(edges):
@@ -102,7 +113,7 @@
         rank.append(jnp.minimum(before, slots - 1))
         group.append(jnp.where(rel_of[e] == 0, 0, rank[e] + 1))
     lane = iota((1, 128), 1)
-    row = jnp.where(lane == COUNT, r.own_s[0, COUNT], 0)
+    row = jnp.zeros((1, 128), jnp.int32)
     for e in range(edges):
         spot = jnp.int32(0)
         for k in range(edges):
@@ -110,11 +121,11 @@
                 spot = spot + (group[k] <= group[e]).astype(jnp.int32)
             elif k > e:
                 spot = spot + (group[k] < group[e]).astype(jnp.int32)
-        goal = r.own_s[0, TARGET + e]
+        goal = r.target_s[e]
         fields = (
             (OWNER, owner[e]),
             (TARGET, goal),
-            (SOURCE, r.own_s[0, SOURCE + e]),
+            (SOURCE, r.source_s[e]),
             (PLACE, jnp.int32(e)),
             (GROUP, group[e]),
             (REL, rel_of[e]),
@@ -125,7 +136,6 @@
     r.row_v[...] = row
     mine = pltpu.make_async_copy(r.row_v, r.row_s, r.l_row)
     mine.start()
-    mine.wait()
 
     pl.semaphore_wait(barrier, n_edge + n_tile - 2)
 
@@ -141,7 +151,7 @@
 
     def meta_copy(rel):
         return remote(
-            r.row_v, r.meta_all.at[me], r.s_meta.at[rel], r.r_meta.at[rel],
+            r.row_v, r.meta_s.at[me], r.s_meta.at[rel], r.r_meta.at[rel],
             (me + rel) % n_edge, tile,
         )
 
@@ -225,16 +235,14 @@
     txt = Halo(FAR, r.text, inner(r.text, FAR), (r.s_tup, r.r_tup, r.s_tdn, r.r_tdn))
 
     each(edges, hid.start)
-    r.meta_all[me] = r.row_v[...]
+    own_row = pltpu.make_async_copy(r.row_v, r.meta_s.at[me], r.l_own)
+    own_row.start()
     for rel in range(1, n_edge):
         remote(
-            r.row_v, r.meta_all.at[(me - rel + n_edge) % n_edge], r.s_meta.at[rel],
+            r.row_v, r.meta_s.at[(me - rel + n_edge) % n_edge], r.s_meta.at[rel],
             r.r_meta.at[rel], (me + rel) % n_edge, tile,
         ).wait_recv()
-    local = pltpu.make_async_copy(r.meta_all, r.meta_s, r.l_meta)
-    local.start()
     loads[0].wait()
-    local.wait()
 
     def feat_copy(rel, s):
         return remote(
@@ -249,6 +257,11 @@
         for rel in range(1, n_edge):
             feat_copy(rel, s).start()
 
+    mine.wait()
+    own_row.wait()
+    tables = pltpu.make_async_copy(r.meta_s, r.meta_all, r.l_meta)
+    tables.start()
+
     def take_source(e):
         r.sext[e, pl.ds(NEAR * width, band)] = r.feat[r.row_s[0, SOURCE + e]]
         src.start(e)
@@ -256,6 +269,9 @@
     each(edges, take_source)
     for halo in (hid, src, txt):
         halo.clear()
+
+    for load in loads[2:]:
+        load.wait()
 
     spot = (iota((128, 64), 0) + 4) & 127
     along = ((spot >> 3) & 3) * 2 + (spot >> 6) - ((spot >> 5) & 1)
@@ -387,7 +403,7 @@
             place = r.row_s[0, PLACE + e]
             state = r.hext[place, pl.ds(NEAR * width, band)]
             fresh = ((1.0 - gate) * state.astype(F32) + gate * candidate).astype(BF)
-            used = (place < r.row_s[0, COUNT]).astype(F32)
+            used = (place < r.count_s[0]).astype(F32)
             live = jnp.full((band, 128), used) > 0.5
             r.held[e] = jnp.where(live, fresh, state)
             heads = nt(r.head_w[...], fresh)
@@ -439,7 +455,7 @@
     blocks = blocks * (1.0 / (MAPH * width))
     of = iota((16, 128), 1) >> 4
     for e in range(edges):
-        used = (r.row_s[0, PLACE + e] < r.row_s[0, COUNT]).astype(jnp.int32)
+        used = (r.row_s[0, PLACE + e] < r.count_s[0]).astype(jnp.int32)
         blocks = jnp.where((of == e) & (jnp.full((16, 128), used) == 0), 0.0, blocks)
     r.gpart[...] = blocks
 
@@ -476,6 +492,7 @@
         ).wait_recv()
 
     store.wait()
+    tables.wait()
     for rel in range(1, n_edge):
         meta_copy(rel).wait_send()
         edge_copy(rel).wait_send()
@@ -577,12 +594,6 @@
     per = edges // slots
     band = rows * width
 
-    fields = (
-        (edge_owner[:, 0], OWNER), (edge_target, TARGET), (edge_source, SOURCE), (edge_counts, COUNT),
-    )
-    meta = jnp.zeros((1, 128), jnp.int32)
-    for field, at in fields:
-        meta = meta + jnp.pad(field, (at, 128 - at - field.shape[0]))[None, :]
     dims = (n_edge, n_tile, edges, frames, rows, width, slots)
     even = (rows + 2 * NEAR + 1) // 2 * 2
     dma = pltpu.SemaphoreType.DMA
@@ -591,22 +602,32 @@
     hbm = pl.BlockSpec(memory_space=pl.ANY)
 
     inputs = (
-        ("own_s", meta, smem),
+        ("owner_h", edge_owner[:, 0], hbm),
+        ("target_h", edge_target, hbm),
+        ("source_h", edge_source, hbm),
+        ("count_h", edge_counts, hbm),
         ("feat_h", features.reshape(frames, band, chan), hbm),
         ("hidden_h", hidden_state.reshape(edges, band, chan), hbm),
-        ("corr_in", corr_weight, vmem),
+        ("corr_h", corr_weight, hbm),
         ("gate_w", gate_weight, hbm),
         ("cand_w", candidate_weight, hbm),
-        ("jac_in", jacobian_weight.T, vmem),
-        ("conf_in", confidence_weight.T, vmem),
+        ("jac_h", jacobian_weight.T, hbm),
+        ("conf_h", confidence_weight.T, hbm),
     )
     outputs = (
         ("out_hidden", (edges, band, chan), BF, hbm),
         ("gall", (n_edge, 16, 128), F32, vmem),
-        ("meta_all", (n_edge, 1, 128), jnp.int32, vmem),
+        ("meta_all", (n_edge, 1, 128), jnp.int32, hbm),
     )
     near, far = len(reach(NEAR, rows)), len(reach(FAR, rows))
     scratch = {
+        "owner_s": pltpu.SMEM((edges,), jnp.int32),
+        "target_s": pltpu.SMEM((edges,), jnp.int32),
+        "source_s": pltpu.SMEM((edges,), jnp.int32),
+        "count_s": pltpu.SMEM((1,), jnp.int32),
+        "corr_in": pltpu.VMEM(corr_weight.shape, BF),
+        "jac_in": pltpu.VMEM(jacobian_weight.shape[::-1], BF),
+        "conf_in": pltpu.VMEM(confidence_weight.shape[::-1], BF),
         "row_v": pltpu.VMEM((1, 128), jnp.int32),
         "row_s": pltpu.SMEM((1, 128), jnp.int32),
         "meta_s": pltpu.SMEM((n_edge, 1, 128), jnp.int32),
@@ -630,10 +651,12 @@
         "gpart": pltpu.VMEM((16, 128), F32),
         "gtile": pltpu.VMEM((n_tile, 16, 128), F32),
         "gsum": pltpu.VMEM((16, 128), F32),
-        "l_in": dma((2,)),
+        "l_in": dma((5,)),
         "l_w": dma((36,)),
+        "l_ints": dma((4,)),
         "l_row": dma,
         "l_meta": dma,
+        "l_own": dma,
         "l_out": dma,
         "s_meta": dma((n_edge,)),
         "r_meta": dma((n_edge,)),

time: 51.6 us -> 49.2 us (0.953)
  other arithmetic: 1.28 us -> 0 us
  Pallas kernels: 48.7 us -> 47.7 us
    add x1 -> x0, other arithmetic: 1.28 us -> none  [per_device(): meta = meta + jnp.pad(field, (at, 128 - at - field.shape[0]))[None, :]]
    pallas_call x1, Pallas kernels: 45.1 us -> 44.1 us  [per_device(): pl.pallas_call(functools.partial(kernel, dims, names), out_shape=tuple((j...]
where the time goes in v4:
time: 49.2 us; the launch traced here: 48.9 us
  Pallas kernels  47.7 us (97%)
  between operations  1.29 us (3%)
    pallas_call x1, Pallas kernels, per_device(): pl.pallas_call(functools.partial(kernel, dims, names), out_shape=tuple((j...  44.1 us
    pallas_call x1, Pallas kernels, per_device(): pl.pallas_call(functools.partial(assemble, dims), out_shape=(jax.ShapeDty...  3.59 us

profile of v4, /device:TPU:0, one launch (start us, length us, event | category | flops | bytes accessed | tf_op | source)
XLA Modules:
  0.0 48.9 jit_solution(6224216859578973332)
XLA Ops:
  1.3 44.1 %shard_map.130 = (bf16[8,384,128]{2,1,0:T(8,128)(2,1)}, f32[4,16,128]{2,1,0:T(8,128)}, s32[4,1,128]{2,1,0:T(1,128)}) custom-call(s32[8]{0:T(128)} %bitcast.9, s32[8]{0:T(128)} %refs_1_.1, s32[8]{0:T(128)} %refs_2_.1, s32[1]{0:T(128)S(6)} %copy.14.refs_3_, bf16[24,384,128]{2,1,0:T(8,128)(2,1)} %bitcast.6, bf16[8,384,128]{2,1,0:T(8,128)(2,1)} %bitcast.7, ...), custom_call_target="tpu_custom_call" | custom-call | tf_op jit(solution)/shard_map/pallas_call | solution.py:676
  45.3 3.6 %shard_map.131 = (bf16[8,384,128]{2,1,0:T(8,128)(2,1)}, f32[72,144]{1,0:T(8,128)}, f32[24,36]{1,0:T(8,128)}) custom-call(s32[4,1,128]{2,1,0:T(1,128)} %get-tuple-element.9.meta_s, f32[4,16,128]{2,1,0:T(8,128)} %get-tuple-element.10.gall, bf16[8,384,128]{2,1,0:T(8,128)(2,1)} %get-tuple-element.11.hidden_h), custom_call_target="tpu_custom_call" | custom-call | tf_op jit(solution)/shard_map/pallas_call | solution.py:686

commit v5 on v4

--- a/solution.py
+++ b/solution.py
@@ -75,19 +75,19 @@
         pltpu.make_async_copy(r.jac_h, r.jac_in, r.l_in.at[3]),
         pltpu.make_async_copy(r.conf_h, r.conf_in, r.l_in.at[4]),
     ]
-    fills = []
-    for a in range(3):
+    first, second = pl.ds(0, 128), pl.ds(128, 128)
+    fills = [
+        pltpu.make_async_copy(r.gate_w.at[:, :, first], r.wh, r.l_w.at[0]),
+        pltpu.make_async_copy(r.gate_w.at[:, :, second], r.wm, r.l_w.at[1]),
+    ]
+    for part, at in enumerate((first, second)):
         for b in range(3):
-            at = pl.ds((a * 3 + b) * 128, 128)
-            first, second = pl.ds(0, 128), pl.ds(128, 128)
-            pairs = (
-                (r.gate_w.at[a, b, first], r.wh.at[at]),
-                (r.gate_w.at[a, b, second], r.wm.at[at]),
-                (r.cand_w.at[a, b, first], r.wc.at[pl.ds(a * 128, 128), pl.ds(b * 128, 128)]),
-                (r.cand_w.at[a, b, second], r.wc.at[pl.ds(384 + a * 128, 128), pl.ds(b * 128, 128)]),
+            fills.append(
+                pltpu.make_async_copy(
+                    r.cand_w.at[:, b, at], r.wc.at[part, :, :, pl.ds(b * 128, 128)], r.l_w.at[2]
+                )
             )
-            for source, target in pairs:
-                fills.append(pltpu.make_async_copy(source, target, r.l_w.at[len(fills)]))
+    filled = fills[:2] + [pltpu.make_async_copy(r.wc, r.wc, r.l_w.at[2])]
     for load in ints + loads + fills:
         load.start()
 
@@ -151,7 +151,7 @@
 
     def meta_copy(rel):
         return remote(
-            r.row_v, r.meta_s.at[me], r.s_meta.at[rel], r.r_meta.at[rel],
+            r.row_v, r.meta_s.at[me], r.s_meta.at[rel - 1], r.r_meta.at[rel - 1],
             (me + rel) % n_edge, tile,
         )
 
@@ -159,38 +159,39 @@
         meta_copy(rel).start()
 
     class Halo:
-        def __init__(self, halo, buf, source, sems):
-            self.halo, self.buf, self.source, self.sems = halo, buf, source, sems
+        def __init__(self, halo, lot, buf, source, sems):
+            self.halo, self.lot, self.buf, self.source, self.sems = halo, lot, buf, source, sems
             self.counts = reach(halo, rows)
 
-        def copies(self, e):
+        def copies(self, i, lot):
+            which = pl.ds(i * lot, lot)
             for d, count in enumerate(self.counts):
                 far, lines = d + 1, count * width
                 s_up, r_up, s_dn, r_dn = self.sems
                 up = remote(
-                    self.source(e, 0, lines),
-                    self.buf.at[e, pl.ds((self.halo + far * rows) * width, lines)],
-                    s_up.at[d, e], r_up.at[d, e], me, tile - far,
+                    self.source(which, 0, lines),
+                    self.buf.at[which, pl.ds((self.halo + far * rows) * width, lines)],
+                    s_up.at[d], r_up.at[d, i], me, tile - far,
                 )
                 dn = remote(
-                    self.source(e, band - lines, lines),
-                    self.buf.at[e, pl.ds((self.halo - d * rows - count) * width, lines)],
-                    s_dn.at[d, e], r_dn.at[d, e], me, tile + far,
+                    self.source(which, band - lines, lines),
+                    self.buf.at[which, pl.ds((self.halo - d * rows - count) * width, lines)],
+                    s_dn.at[d], r_dn.at[d, i], me, tile + far,
                 )
                 yield tile >= far, tile + far < n_tile, up, dn
 
-        def start(self, e):
-            for above, below, up, dn in self.copies(e):
+        def start(self, i):
+            for above, below, up, dn in self.copies(i, self.lot):
                 pl.when(above)(up.start)
                 pl.when(below)(dn.start)
 
-        def received(self, e):
-            for above, below, up, dn in self.copies(e):
+        def received(self, i):
+            for above, below, up, dn in self.copies(i, self.lot):
                 pl.when(below)(up.wait_recv)
                 pl.when(above)(dn.wait_recv)
 
-        def sent(self, e):
-            for above, below, up, dn in self.copies(e):
+        def sent(self):
+            for above, below, up, dn in self.copies(0, edges):
                 pl.when(above)(up.wait_send)
                 pl.when(below)(dn.wait_send)
 
@@ -225,35 +226,45 @@
                 each(edges, clear_pad)
 
     def inner(buf, halo):
-        return lambda e, at, lines: buf.at[e, pl.ds(halo * width + at, lines)]
+        return lambda which, at, lines: buf.at[which, pl.ds(halo * width + at, lines)]
 
     hid = Halo(
-        NEAR, r.hext, lambda e, at, lines: r.hidden_h.at[e, pl.ds(at, lines)],
+        NEAR, edges, r.hext, lambda which, at, lines: r.hidden_h.at[which, pl.ds(at, lines)],
         (r.s_hup, r.r_hup, r.s_hdn, r.r_hdn),
     )
-    src = Halo(NEAR, r.sext, inner(r.sext, NEAR), (r.s_sup, r.r_sup, r.s_sdn, r.r_sdn))
-    txt = Halo(FAR, r.text, inner(r.text, FAR), (r.s_tup, r.r_tup, r.s_tdn, r.r_tdn))
-
-    each(edges, hid.start)
+    src = Halo(
+        NEAR, edges, r.sext, inner(r.sext, NEAR), (r.s_sup, r.r_sup, r.s_sdn, r.r_sdn)
+    )
+    txt = Halo(FAR, 1, r.text, inner(r.text, FAR), (r.s_tup, r.r_tup, r.s_tdn, r.r_tdn))
+
+    hid.start(0)
     own_row = pltpu.make_async_copy(r.row_v, r.meta_s.at[me], r.l_own)
     own_row.start()
     for rel in range(1, n_edge):
         remote(
-            r.row_v, r.meta_s.at[(me - rel + n_edge) % n_edge], r.s_meta.at[rel],
-            r.r_meta.at[rel], (me + rel) % n_edge, tile,
+            r.row_v, r.meta_s.at[(me - rel + n_edge) % n_edge], r.s_meta.at[rel - 1],
+            r.r_meta.at[rel - 1], (me + rel) % n_edge, tile,
         ).wait_recv()
     loads[0].wait()
 
+    others = n_edge - 1
+
     def feat_copy(rel, s):
         return remote(
-            r.send.at[(rel - 1) * slots + s], texts[s].at[rel - 1],
-            r.s_feat.at[rel, s], r.r_feat.at[rel, s], (me - rel + n_edge) % n_edge, tile,
+            r.send.at[s * others + rel - 1], texts[s].at[rel - 1],
+            r.s_feat, r.r_feat.at[s], (me - rel + n_edge) % n_edge, tile,
+        )
+
+    def feat_group(s):
+        return remote(
+            r.send.at[pl.ds(s * others, others)], texts[s],
+            r.s_feat, r.r_feat.at[s], (me + 1) % n_edge, tile,
         )
 
     for s in range(slots):
         for rel in range(1, n_edge):
             peer = (me - rel + n_edge) % n_edge
-            r.send[(rel - 1) * slots + s] = r.feat[r.meta_s[peer, 0, ASKS + rel * slots + s]]
+            r.send[s * others + rel - 1] = r.feat[r.meta_s[peer, 0, ASKS + rel * slots + s]]
         for rel in range(1, n_edge):
             feat_copy(rel, s).start()
 
@@ -264,9 +275,9 @@
 
     def take_source(e):
         r.sext[e, pl.ds(NEAR * width, band)] = r.feat[r.row_s[0, SOURCE + e]]
-        src.start(e)
 
     each(edges, take_source)
+    src.start(0)
     for halo in (hid, src, txt):
         halo.clear()
 
@@ -325,14 +336,39 @@
         for q in range(per):
             e = p * per + q
             spread(r.hext[r.row_s[0, PLACE + e]], r.x3.at[q])
-            r.gpre[e] = nn(windows(r.x3, q, rows + 2), r.wh[...])
+            r.gpre[e] = nn(windows(r.x3, q, rows + 2), r.wh[...].reshape(9 * 128, 256))
 
     loads[1].wait()
-    for fill in fills:
+    for fill in filled:
         fill.wait()
-    each(edges, hid.received)
-    each(slots, state_part)
-    each(edges, src.received)
+    flip_row, flip_col = iota((2 * width, 2 * width), 0), iota((2 * width, 2 * width), 1)
+    flip = one_hot(
+        (flip_row // width == flip_col // width)
+        & ((flip_row & (width - 1)) + (flip_col & (width - 1)) == width - 1)
+    )
+
+    def take_target(e, upto):
+        value = r.feat[r.row_s[0, TARGET + e]]
+        at = jnp.maximum(r.row_s[0, REL + e] - 1, 0)
+        for s in range(upto + 1):
+            value = jnp.where(r.row_s[0, GROUP + e] == s + 1, texts[s][at], value)
+        for first in range(0, band, 2 * width):
+            count = min(2 * width, band - first)
+            r.text[e, pl.ds(FAR * width + first, count)] = nn(
+                flip[0:count, 0:count], value[first : first + count]
+            ).astype(BF)
+        txt.start(e)
+
+    def take(s):
+        feat_group(s).wait_recv()
+        for q in range(per):
+            take_target(s * per + q, s)
+
+    hid.received(0)
+    each(slots // 2, state_part)
+    take(0)
+    each(slots - slots // 2, lambda p: state_part(p + slots // 2))
+    src.received(0)
 
     lane_w = (iota((width, 128), 1) + 4) & 127
     col_w = iota((width, 128), 0) + RADIUS - (lane_w & 7)
@@ -378,7 +414,7 @@
             motion_of(p * per + q, q)
         for q in range(per):
             e = p * per + q
-            before = r.gpre[e] + nn(windows(r.x3, q, rows + 2), r.wm[...])
+            before = r.gpre[e] + nn(windows(r.x3, q, rows + 2), r.wm[...].reshape(9 * 128, 256))
             r.upd[q] = 0.5 * jnp.tanh(0.5 * before[width : width + band, 0:128]) + 0.5
             reset = 0.5 * jnp.tanh(0.5 * before[:, 128:256]) + 0.5
             state = r.hext[r.row_s[0, PLACE + e], pl.ds(width, wide_band)].astype(F32)
@@ -394,7 +430,7 @@
                     ],
                     axis=1,
                 ),
-                r.wc[...],
+                r.wc[...].reshape(6 * 128, 384),
             )
             candidate = jnp.tanh(
                 nudge(part[:, 0:128], 1) + part[:, 128:256] + nudge(part[:, 256:384], -1)
@@ -413,37 +449,16 @@
             r.jall[at16] = jnp.concatenate([jac[0:16], jac[16:32]], axis=1).astype(BF)
             r.wall[at16] = jnp.concatenate([weighted[0:16], weighted[16:32]], axis=1).astype(BF)
 
-    flip_row, flip_col = iota((2 * width, 2 * width), 0), iota((2 * width, 2 * width), 1)
-    flip = one_hot(
-        (flip_row // width == flip_col // width)
-        & ((flip_row & (width - 1)) + (flip_col & (width - 1)) == width - 1)
-    )
-
-    def take_target(e, upto):
-        value = r.feat[r.row_s[0, TARGET + e]]
-        at = jnp.maximum(r.row_s[0, REL + e] - 1, 0)
-        for s in range(upto + 1):
-            value = jnp.where(r.row_s[0, GROUP + e] == s + 1, texts[s][at], value)
-        for first in range(0, band, 2 * width):
-            count = min(2 * width, band - first)
-            r.text[e, pl.ds(FAR * width + first, count)] = nn(
-                flip[0:count, 0:count], value[first : first + count]
-            ).astype(BF)
-        txt.start(e)
-
     def stage(p):
-        for s in range(slots):
-
-            @pl.when(p == s)
+        for s in range(1, slots):
+
+            @pl.when(p == s - 1)
             def _():
-                for rel in range(1, n_edge):
-                    feat_copy(rel, s).wait_recv()
-                for q in range(per):
-                    take_target(s * per + q, s)
-
-        pl.when(p > 0)(lambda: update(p - 1))
-
-    each(slots + 1, stage)
+                take(s)
+
+        update(p)
+
+    each(slots, stage)
     store = pltpu.make_async_copy(r.held, r.out_hidden, r.l_out)
     store.start()
 
@@ -461,47 +476,44 @@
 
     def tile_copy(rel):
         return remote(
-            r.gpart, r.gtile.at[tile], r.s_gt.at[rel], r.r_gt.at[rel], me, (tile + rel) % n_tile
-        )
+            r.gpart, r.gtile.at[tile], r.s_gt, r.r_gt, me, (tile + rel) % n_tile
+        )
+
+    def all_tiles():
+        some = r.gtile.at[pl.ds(0, n_tile - 1)]
+        return remote(some, some, r.s_gt, r.r_gt, me, (tile + 1) % n_tile)
 
     for rel in range(1, n_tile):
         tile_copy(rel).start()
     r.gtile[tile] = r.gpart[...]
-    for rel in range(1, n_tile):
-        remote(
-            r.gpart, r.gtile.at[(tile - rel + n_tile) % n_tile], r.s_gt.at[rel], r.r_gt.at[rel],
-            me, (tile + rel) % n_tile,
-        ).wait_recv()
+    all_tiles().wait_recv()
     total = r.gtile[0]
     for k in range(1, n_tile):
         total = total + r.gtile[k]
     r.gsum[...] = total
 
     def edge_copy(rel):
-        return remote(
-            r.gsum, r.gall.at[me], r.s_ge.at[rel], r.r_ge.at[rel], (me + rel) % n_edge, tile
-        )
+        return remote(r.gsum, r.gall.at[me], r.s_ge, r.r_ge, (me + rel) % n_edge, tile)
+
+    def all_edges():
+        some = r.gall.at[pl.ds(0, others)]
+        return remote(some, some, r.s_ge, r.r_ge, (me + 1) % n_edge, tile)
 
     for rel in range(1, n_edge):
         edge_copy(rel).start()
     r.gall[me] = total
-    for rel in range(1, n_edge):
-        remote(
-            r.gsum, r.gall.at[(me - rel + n_edge) % n_edge], r.s_ge.at[rel], r.r_ge.at[rel],
-            (me + rel) % n_edge, tile,
-        ).wait_recv()
+    all_edges().wait_recv()
 
     store.wait()
     tables.wait()
     for rel in range(1, n_edge):
         meta_copy(rel).wait_send()
-        edge_copy(rel).wait_send()
-        for s in range(slots):
-            feat_copy(rel, s).wait_send()
-    for rel in range(1, n_tile):
-        tile_copy(rel).wait_send()
+    for s in range(slots):
+        feat_group(s).wait_send()
+    all_tiles().wait_send()
+    all_edges().wait_send()
     for halo in (hid, src, txt):
-        each(edges, halo.sent)
+        halo.sent()
 
 
 def halves(value):
@@ -513,7 +525,7 @@
     n_edge, n_tile, edges, frames, rows, width, slots = dims
     me = lax.axis_index("edge")
     tile = lax.axis_index("tile")
-    fetch = pltpu.make_async_copy(hidden_h, held, sem.at[edges])
+    fetch = pltpu.make_async_copy(hidden_h, held, sem.at[0])
     fetch.start()
     cam_rows, cam_cols = out_cam.shape
     row_id = iota((cam_rows, 128), 0) + tile * cam_rows
@@ -543,7 +555,7 @@
     placed = nt(jnp.concatenate(lefts + lows, axis=1), jnp.concatenate(rights + rights, axis=1))
     fetch.wait()
     stores = [
-        pltpu.make_async_copy(held.at[e], out_hidden.at[meta_s[me, 0, PLACE + e]], sem.at[e])
+        pltpu.make_async_copy(held.at[e], out_hidden.at[meta_s[me, 0, PLACE + e]], sem.at[1])
         for e in range(edges)
     ]
     for store in stores:
@@ -569,8 +581,7 @@
     )
     high, low = halves(spread)
     out_diag[...] = (nn(fold, high) + nn(fold, low))[:, 0:36]
-    for store in stores:
-        store.wait()
+    pltpu.make_async_copy(held, out_hidden, sem.at[1]).wait()
 
 
 def per_device(
@@ -639,9 +650,9 @@
         "hext": pltpu.VMEM((edges, (rows + 2 * NEAR) * width, chan), BF),
         "rext": pltpu.VMEM((per, (rows + 2) * width, chan), BF),
         "x3": pltpu.VMEM((per, (rows + 2 * NEAR) * width, 3 * chan), BF),
-        "wh": pltpu.VMEM((9 * chan, 2 * chan), BF),
-        "wm": pltpu.VMEM((9 * chan, 2 * chan), BF),
-        "wc": pltpu.VMEM((6 * chan, 3 * chan), BF),
+        "wh": pltpu.VMEM((3, 3, chan, 2 * chan), BF),
+        "wm": pltpu.VMEM((3, 3, chan, 2 * chan), BF),
+        "wc": pltpu.VMEM((2, 3, chan, 3 * chan), BF),
         "corr_w": pltpu.VMEM((128, chan), BF),
         "head_w": pltpu.VMEM((64, chan), BF),
         "gpre": pltpu.VMEM((edges, (rows + 2) * width, 2 * chan), F32),
@@ -652,26 +663,27 @@
         "gtile": pltpu.VMEM((n_tile, 16, 128), F32),
         "gsum": pltpu.VMEM((16, 128), F32),
         "l_in": dma((5,)),
-        "l_w": dma((36,)),
+        "l_w": dma((3,)),
         "l_ints": dma((4,)),
         "l_row": dma,
         "l_meta": dma,
         "l_own": dma,
         "l_out": dma,
-        "s_meta": dma((n_edge,)),
-        "r_meta": dma((n_edge,)),
-        "s_feat": dma((n_edge, slots)),
-        "r_feat": dma((n_edge, slots)),
-        "s_gt": dma((n_tile,)),
-        "r_gt": dma((n_tile,)),
-        "s_ge": dma((n_edge,)),
-        "r_ge": dma((n_edge,)),
+        "s_meta": dma((n_edge - 1,)),
+        "r_meta": dma((n_edge - 1,)),
+        "s_feat": dma,
+        "r_feat": dma((slots,)),
+        "s_gt": dma,
+        "r_gt": dma,
+        "s_ge": dma,
+        "r_ge": dma,
     }
     for s in range(slots):
         scratch[f"text{s}"] = pltpu.VMEM((n_edge - 1, band, chan), BF)
-    for key, count in (("h", near), ("s", near), ("t", far)):
-        for name in (f"s_{key}up", f"r_{key}up", f"s_{key}dn", f"r_{key}dn"):
-            scratch[name] = dma((count, edges))
+    for key, count, lots in (("h", near, 1), ("s", near, 1), ("t", far, edges)):
+        for way in ("up", "dn"):
+            scratch[f"s_{key}{way}"] = dma((count,))
+            scratch[f"r_{key}{way}"] = dma((count, lots))
     names = [i[0] for i in inputs] + [o[0] for o in outputs] + list(scratch)
     state, gall, meta_all = pl.pallas_call(
         functools.partial(kernel, dims, names),
@@ -692,7 +704,7 @@
         ),
         in_specs=[smem, vmem, hbm],
         out_specs=(hbm, vmem, vmem),
-        scratch_shapes=[pltpu.VMEM((edges, band, chan), BF), dma((edges + 1,))],
+        scratch_shapes=[pltpu.VMEM((edges, band, chan), BF), dma((2,))],
     )(meta_all, gall, state)
     return hidden_next.reshape(hidden_state.shape), cam, diag
 

time: 49.2 us -> 47.5 us (0.965)
  Pallas kernels: 47.7 us -> 45.9 us
    pallas_call x1, Pallas kernels: 44.1 us -> 42.4 us  [per_device(): pl.pallas_call(functools.partial(kernel, dims, names), out_shape=tuple((j...]
where the time goes in v5:
time: 47.5 us; the launch traced here: 47.2 us
  Pallas kernels  45.9 us (97%)
  between operations  1.29 us (3%)
    pallas_call x1, Pallas kernels, per_device(): pl.pallas_call(functools.partial(kernel, dims, names), out_shape=tuple((j...  42.4 us
    pallas_call x1, Pallas kernels, per_device(): pl.pallas_call(functools.partial(assemble, dims), out_shape=(jax.ShapeDty...  3.53 us

profile of v5, /device:TPU:0, one launch (start us, length us, event | category | flops | bytes accessed | tf_op | source)
XLA Modules:
  0.0 47.2 jit_solution(1307733912606841949)
XLA Ops:
  1.3 42.4 %shard_map.130 = (bf16[8,384,128]{2,1,0:T(8,128)(2,1)}, f32[4,16,128]{2,1,0:T(8,128)}, s32[4,1,128]{2,1,0:T(1,128)}) custom-call(s32[8]{0:T(128)} %bitcast.9, s32[8]{0:T(128)} %refs_1_.1, s32[8]{0:T(128)} %refs_2_.1, s32[1]{0:T(128)S(6)} %copy.14.refs_3_, bf16[24,384,128]{2,1,0:T(8,128)(2,1)} %bitcast.6, bf16[8,384,128]{2,1,0:T(8,128)(2,1)} %bitcast.7, ...), custom_call_target="tpu_custom_call" | custom-call | tf_op jit(solution)/shard_map/pallas_call | solution.py:688
  43.7 3.5 %shard_map.131 = (bf16[8,384,128]{2,1,0:T(8,128)(2,1)}, f32[72,144]{1,0:T(8,128)}, f32[24,36]{1,0:T(8,128)}) custom-call(s32[4,1,128]{2,1,0:T(1,128)} %get-tuple-element.9.meta_s, f32[4,16,128]{2,1,0:T(8,128)} %get-tuple-element.10.gall, bf16[8,384,128]{2,1,0:T(8,128)(2,1)} %get-tuple-element.11.hidden_h), custom_call_target="tpu_custom_call" | custom-call | tf_op jit(solution)/shard_map/pallas_call | solution.py:698

commit v6 on v5

--- a/solution.py
+++ b/solution.py
@@ -13,7 +13,7 @@
 RADIUS = WINDOW // 2
 NEAR = 2
 FAR = RADIUS + NEAR
-OWNER, TARGET, SOURCE, PLACE, GROUP, REL, ASKS = 0, 8, 16, 32, 40, 48, 64
+OWNER, TARGET, SOURCE, SPOT, PLACE, GROUP, REL = 0, 8, 16, 24, 32, 40, 48
 MESH = pl.DeviceIdType.MESH
 BF = jnp.bfloat16
 F32 = jnp.float32
@@ -101,6 +101,155 @@
             barrier, inc=1, device_id=(me, (tile + rel) % n_tile), device_id_type=MESH
         )
 
+    pl.semaphore_wait(barrier, n_edge + n_tile - 2)
+
+    def remote(src, dst, send_sem, recv_sem, edge_id, tile_id):
+        return pltpu.make_async_remote_copy(
+            src_ref=src,
+            dst_ref=dst,
+            send_sem=send_sem,
+            recv_sem=recv_sem,
+            device_id=(edge_id, tile_id),
+            device_id_type=MESH,
+        )
+
+    def meta_copy(rel):
+        return remote(
+            r.row_v, r.meta_s.at[me], r.s_meta.at[rel - 1], r.r_meta.at[rel - 1],
+            (me + rel) % n_edge, tile,
+        )
+
+    others = n_edge - 1
+    raws = (r.owner_h, r.target_h)
+
+    def raw_copy(k, rel):
+        return remote(
+            raws[k], r.raw_s.at[k, me], r.s_raw.at[k, rel - 1], r.r_raw.at[k, rel - 1],
+            (me + rel) % n_edge, tile,
+        )
+
+    for rel in range(1, n_edge):
+        for k in range(2):
+            raw_copy(k, rel).start()
+
+    class Halo:
+        def __init__(self, halo, lot, buf, source, sems):
+            self.halo, self.lot, self.buf, self.source, self.sems = halo, lot, buf, source, sems
+            self.counts = reach(halo, rows)
+
+        def copies(self, i, lot):
+            which = pl.ds(i * lot, lot)
+            for d, count in enumerate(self.counts):
+                far, lines = d + 1, count * width
+                s_up, r_up, s_dn, r_dn = self.sems
+                up = remote(
+                    self.source(which, 0, lines),
+                    self.buf.at[which, pl.ds((self.halo + far * rows) * width, lines)],
+                    s_up.at[d], r_up.at[d, i], me, tile - far,
+                )
+                dn = remote(
+                    self.source(which, band - lines, lines),
+                    self.buf.at[which, pl.ds((self.halo - d * rows - count) * width, lines)],
+                    s_dn.at[d], r_dn.at[d, i], me, tile + far,
+                )
+                yield tile >= far, tile + far < n_tile, up, dn
+
+        def start(self, i):
+            for above, below, up, dn in self.copies(i, self.lot):
+                pl.when(above)(up.start)
+                pl.when(below)(dn.start)
+
+        def received(self, i):
+            for above, below, up, dn in self.copies(i, self.lot):
+                pl.when(below)(up.wait_recv)
+                pl.when(above)(dn.wait_recv)
+
+        def sent(self):
+            for above, below, up, dn in self.copies(0, edges):
+                pl.when(above)(up.wait_send)
+                pl.when(below)(dn.wait_send)
+
+        def clear(self):
+            for d, count in enumerate(self.counts):
+                far, lines = d + 1, count * width
+                zero = jnp.zeros((lines, 128), BF)
+                top = (self.halo - d * rows - count) * width
+                low = (self.halo + far * rows) * width
+
+                @pl.when(tile < far)
+                def _():
+                    def clear_top(e):
+                        self.buf[e, pl.ds(top, lines)] = zero
+
+                    each(edges, clear_top)
+
+                @pl.when(tile + far >= n_tile)
+                def _():
+                    def clear_low(e):
+                        self.buf[e, pl.ds(low, lines)] = zero
+
+                    each(edges, clear_low)
+
+            used = (rows + 2 * self.halo) * width
+            spare = self.buf.shape[1] - used
+            if spare:
+
+                def clear_pad(e):
+                    self.buf[e, pl.ds(used, spare)] = jnp.zeros((spare, 128), BF)
+
+                each(edges, clear_pad)
+
+    def inner(buf, halo):
+        return lambda which, at, lines: buf.at[which, pl.ds(halo * width + at, lines)]
+
+    hid = Halo(
+        NEAR, edges, r.hext, lambda which, at, lines: r.hidden_h.at[which, pl.ds(at, lines)],
+        (r.s_hup, r.r_hup, r.s_hdn, r.r_hdn),
+    )
+    src = Halo(
+        NEAR, edges, r.sext, inner(r.sext, NEAR), (r.s_sup, r.r_sup, r.s_sdn, r.r_sdn)
+    )
+    txt = Halo(FAR, 1, r.text, inner(r.text, FAR), (r.s_tup, r.r_tup, r.s_tdn, r.r_tdn))
+
+    hid.start(0)
+    for rel in range(1, n_edge):
+        for k in range(2):
+            remote(
+                raws[k], r.raw_s.at[k, (me - rel + n_edge) % n_edge], r.s_raw.at[k, rel - 1],
+                r.r_raw.at[k, rel - 1], (me + rel) % n_edge, tile,
+            ).wait_recv()
+    loads[0].wait()
+
+    def asked(peer):
+        picks, count = [jnp.int32(0)] * slots, jnp.int32(0)
+        for k in range(edges):
+            hit = (r.raw_s[0, peer, k] == me).astype(jnp.int32)
+            goal = r.raw_s[1, peer, k]
+            for s in range(slots):
+                picks[s] = jnp.where((hit == 1) & (count == s), goal, picks[s])
+            count = count + hit
+        return picks
+
+    asks = [asked((me - rel + n_edge) % n_edge) for rel in range(1, n_edge)]
+
+    def feat_copy(rel, s):
+        return remote(
+            r.send.at[s * others + rel - 1], texts[s].at[rel - 1],
+            r.s_feat, r.r_feat.at[s], (me - rel + n_edge) % n_edge, tile,
+        )
+
+    def feat_group(s):
+        return remote(
+            r.send.at[pl.ds(s * others, others)], texts[s],
+            r.s_feat, r.r_feat.at[s], (me + 1) % n_edge, tile,
+        )
+
+    for s in range(slots):
+        for rel in range(1, n_edge):
+            r.send[s * others + rel - 1] = r.feat[asks[rel - 1][s]]
+        for rel in range(1, n_edge):
+            feat_copy(rel, s).start()
+
     for load in ints:
         load.wait()
     owner = [r.owner_s[e] for e in range(edges)]
@@ -132,146 +281,15 @@
         )
         for base, value in fields:
             row = jnp.where(lane == base + spot, value, row)
-        row = jnp.where(lane == ASKS + rel_of[e] * slots + rank[e], goal, row)
+        row = jnp.where(lane == SPOT + e, spot, row)
     r.row_v[...] = row
     mine = pltpu.make_async_copy(r.row_v, r.row_s, r.l_row)
     mine.start()
-
-    pl.semaphore_wait(barrier, n_edge + n_tile - 2)
-
-    def remote(src, dst, send_sem, recv_sem, edge_id, tile_id):
-        return pltpu.make_async_remote_copy(
-            src_ref=src,
-            dst_ref=dst,
-            send_sem=send_sem,
-            recv_sem=recv_sem,
-            device_id=(edge_id, tile_id),
-            device_id_type=MESH,
-        )
-
-    def meta_copy(rel):
-        return remote(
-            r.row_v, r.meta_s.at[me], r.s_meta.at[rel - 1], r.r_meta.at[rel - 1],
-            (me + rel) % n_edge, tile,
-        )
-
     for rel in range(1, n_edge):
         meta_copy(rel).start()
-
-    class Halo:
-        def __init__(self, halo, lot, buf, source, sems):
-            self.halo, self.lot, self.buf, self.source, self.sems = halo, lot, buf, source, sems
-            self.counts = reach(halo, rows)
-
-        def copies(self, i, lot):
-            which = pl.ds(i * lot, lot)
-            for d, count in enumerate(self.counts):
-                far, lines = d + 1, count * width
-                s_up, r_up, s_dn, r_dn = self.sems
-                up = remote(
-                    self.source(which, 0, lines),
-                    self.buf.at[which, pl.ds((self.halo + far * rows) * width, lines)],
-                    s_up.at[d], r_up.at[d, i], me, tile - far,
-                )
-                dn = remote(
-                    self.source(which, band - lines, lines),
-                    self.buf.at[which, pl.ds((self.halo - d * rows - count) * width, lines)],
-                    s_dn.at[d], r_dn.at[d, i], me, tile + far,
-                )
-                yield tile >= far, tile + far < n_tile, up, dn
-
-        def start(self, i):
-            for above, below, up, dn in self.copies(i, self.lot):
-                pl.when(above)(up.start)
-                pl.when(below)(dn.start)
-
-        def received(self, i):
-            for above, below, up, dn in self.copies(i, self.lot):
-                pl.when(below)(up.wait_recv)
-                pl.when(above)(dn.wait_recv)
-
-        def sent(self):
-            for above, below, up, dn in self.copies(0, edges):
-                pl.when(above)(up.wait_send)
-                pl.when(below)(dn.wait_send)
-
-        def clear(self):
-            for d, count in enumerate(self.counts):
-                far, lines = d + 1, count * width
-                zero = jnp.zeros((lines, 128), BF)
-                top = (self.halo - d * rows - count) * width
-                low = (self.halo + far * rows) * width
-
-                @pl.when(tile < far)
-                def _():
-                    def clear_top(e):
-                        self.buf[e, pl.ds(top, lines)] = zero
-
-                    each(edges, clear_top)
-
-                @pl.when(tile + far >= n_tile)
-                def _():
-                    def clear_low(e):
-                        self.buf[e, pl.ds(low, lines)] = zero
-
-                    each(edges, clear_low)
-
-            used = (rows + 2 * self.halo) * width
-            spare = self.buf.shape[1] - used
-            if spare:
-
-                def clear_pad(e):
-                    self.buf[e, pl.ds(used, spare)] = jnp.zeros((spare, 128), BF)
-
-                each(edges, clear_pad)
-
-    def inner(buf, halo):
-        return lambda which, at, lines: buf.at[which, pl.ds(halo * width + at, lines)]
-
-    hid = Halo(
-        NEAR, edges, r.hext, lambda which, at, lines: r.hidden_h.at[which, pl.ds(at, lines)],
-        (r.s_hup, r.r_hup, r.s_hdn, r.r_hdn),
-    )
-    src = Halo(
-        NEAR, edges, r.sext, inner(r.sext, NEAR), (r.s_sup, r.r_sup, r.s_sdn, r.r_sdn)
-    )
-    txt = Halo(FAR, 1, r.text, inner(r.text, FAR), (r.s_tup, r.r_tup, r.s_tdn, r.r_tdn))
-
-    hid.start(0)
     own_row = pltpu.make_async_copy(r.row_v, r.meta_s.at[me], r.l_own)
     own_row.start()
-    for rel in range(1, n_edge):
-        remote(
-            r.row_v, r.meta_s.at[(me - rel + n_edge) % n_edge], r.s_meta.at[rel - 1],
-            r.r_meta.at[rel - 1], (me + rel) % n_edge, tile,
-        ).wait_recv()
-    loads[0].wait()
-
-    others = n_edge - 1
-
-    def feat_copy(rel, s):
-        return remote(
-            r.send.at[s * others + rel - 1], texts[s].at[rel - 1],
-            r.s_feat, r.r_feat.at[s], (me - rel + n_edge) % n_edge, tile,
-        )
-
-    def feat_group(s):
-        return remote(
-            r.send.at[pl.ds(s * others, others)], texts[s],
-            r.s_feat, r.r_feat.at[s], (me + 1) % n_edge, tile,
-        )
-
-    for s in range(slots):
-        for rel in range(1, n_edge):
-            peer = (me - rel + n_edge) % n_edge
-            r.send[s * others + rel - 1] = r.feat[r.meta_s[peer, 0, ASKS + rel * slots + s]]
-        for rel in range(1, n_edge):
-            feat_copy(rel, s).start()
-
     mine.wait()
-    own_row.wait()
-    tables = pltpu.make_async_copy(r.meta_s, r.meta_all, r.l_meta)
-    tables.start()
 
     def take_source(e):
         r.sext[e, pl.ds(NEAR * width, band)] = r.feat[r.row_s[0, SOURCE + e]]
@@ -369,6 +387,32 @@
     take(0)
     each(slots - slots // 2, lambda p: state_part(p + slots // 2))
     src.received(0)
+
+    own_row.wait()
+    for rel in range(1, n_edge):
+        remote(
+            r.row_v, r.meta_s.at[(me - rel + n_edge) % n_edge], r.s_meta.at[rel - 1],
+            r.r_meta.at[rel - 1], (me + rel) % n_edge, tile,
+        ).wait_recv()
+    cam_cols = frames * 6
+    cam_rows = r.where_v.shape[1] - cam_cols
+    part = iota((cam_rows + cam_cols, 128), 0)
+    index = jnp.where(part < cam_rows, part + tile * cam_rows, part - cam_rows + me * cam_cols)
+    inside = lane & 15
+    digit = jnp.where(inside < 6, inside, inside - 6)
+
+    def place(j):
+        spots = jnp.full((1, 128), -1, jnp.int32)
+        for e in range(edges):
+            source = (j * frames + r.meta_s[j, 0, SOURCE + e]) * 6
+            target = (r.meta_s[j, 0, OWNER + e] * frames + r.meta_s[j, 0, TARGET + e]) * 6
+            here = jnp.where(inside < 6, source, target) + digit
+            spots = jnp.where(((lane >> 4) == e) & (inside < 12), here, spots)
+        r.where_v[j] = one_hot(index == spots)
+
+    each(n_edge, place)
+    tables = pltpu.make_async_copy(r.where_v, r.where_h, r.l_meta)
+    tables.start()
 
     lane_w = (iota((width, 128), 1) + 4) & 127
     col_w = iota((width, 128), 0) + RADIUS - (lane_w & 7)
@@ -459,9 +503,6 @@
         update(p)
 
     each(slots, stage)
-    store = pltpu.make_async_copy(r.held, r.out_hidden, r.l_out)
-    store.start()
-
     same = (iota((128, 128), 0) >> 4) == (iota((128, 128), 1) >> 4)
     square = jnp.where(same, nt(r.wall[...], r.jall[...]), 0.0)
     blocks = square[0:16]
@@ -486,6 +527,13 @@
     for rel in range(1, n_tile):
         tile_copy(rel).start()
     r.gtile[tile] = r.gpart[...]
+
+    def put_back(e):
+        r.ready[e] = r.held[r.row_s[0, SPOT + e]]
+
+    each(edges, put_back)
+    store = pltpu.make_async_copy(r.ready, r.out_hidden, r.l_out)
+    store.start()
     all_tiles().wait_recv()
     total = r.gtile[0]
     for k in range(1, n_tile):
@@ -508,6 +556,8 @@
     tables.wait()
     for rel in range(1, n_edge):
         meta_copy(rel).wait_send()
+        for k in range(2):
+            raw_copy(k, rel).wait_send()
     for s in range(slots):
         feat_group(s).wait_send()
     all_tiles().wait_send()
@@ -521,29 +571,17 @@
     return high, (value - high.astype(F32)).astype(BF)
 
 
-def assemble(dims, meta_s, gall, hidden_h, out_hidden, out_cam, out_diag, held, sem):
+def assemble(dims, where_v, gall, hidden_h, out_hidden, out_cam, out_diag, held, sem):
     n_edge, n_tile, edges, frames, rows, width, slots = dims
     me = lax.axis_index("edge")
     tile = lax.axis_index("tile")
     fetch = pltpu.make_async_copy(hidden_h, held, sem.at[0])
     fetch.start()
     cam_rows, cam_cols = out_cam.shape
-    row_id = iota((cam_rows, 128), 0) + tile * cam_rows
-    col_id = iota((cam_cols, 128), 0) + me * cam_cols
     same = (iota((128, 128), 0) >> 4) == (iota((128, 128), 1) >> 4)
-    lane = iota((1, 128), 1)
-    inner = lane & 15
-    digit = jnp.where(inner < 6, inner, inner - 6)
     lefts, lows, rights = [], [], []
     for j in range(n_edge):
-        spots = jnp.full((1, 128), -1, jnp.int32)
-        for e in range(edges):
-            source = (j * frames + meta_s[j, 0, SOURCE + e]) * 6
-            target = (meta_s[j, 0, OWNER + e] * frames + meta_s[j, 0, TARGET + e]) * 6
-            here = jnp.where(inner < 6, source, target) + digit
-            spots = jnp.where(((lane >> 4) == e) & (inner < 12), here, spots)
-        mine = (col_id == spots).astype(F32)
-        left = jnp.concatenate([(row_id == spots).astype(F32), mine], axis=0).astype(BF)
+        left = where_v[j]
         stack = jnp.where(same, jnp.concatenate([gall[j]] * 8, axis=0), 0.0)
         picked = nn(
             jnp.concatenate([left, left], axis=1), jnp.concatenate(halves(stack), axis=0)
@@ -551,15 +589,11 @@
         high, low = halves(picked)
         lefts.append(high)
         lows.append(low)
-        rights.append(mine.astype(BF))
+        rights.append(left[cam_rows:])
     placed = nt(jnp.concatenate(lefts + lows, axis=1), jnp.concatenate(rights + rights, axis=1))
     fetch.wait()
-    stores = [
-        pltpu.make_async_copy(held.at[e], out_hidden.at[meta_s[me, 0, PLACE + e]], sem.at[1])
-        for e in range(edges)
-    ]
-    for store in stores:
-        store.start()
+    store = pltpu.make_async_copy(held, out_hidden, sem.at[1])
+    store.start()
     cam = placed[0:cam_rows]
     row_frame = sixth(iota((cam_rows, cam_cols), 0) + tile * cam_rows)
     col_frame = sixth(iota((cam_rows, cam_cols), 1) + me * cam_cols)
@@ -581,7 +615,7 @@
     )
     high, low = halves(spread)
     out_diag[...] = (nn(fold, high) + nn(fold, low))[:, 0:36]
-    pltpu.make_async_copy(held, out_hidden, sem.at[1]).wait()
+    store.wait()
 
 
 def per_device(
@@ -601,7 +635,7 @@
     edges = hidden_state.shape[0]
     frames, rows, width, chan = features.shape
     slots = max(2, (2 * edges + n_edge - 1) // n_edge)
-    assert edges % slots == 0 and edges <= 8 and ASKS + n_edge * slots <= 128
+    assert edges % slots == 0 and edges <= 8
     per = edges // slots
     band = rows * width
 
@@ -609,7 +643,6 @@
     even = (rows + 2 * NEAR + 1) // 2 * 2
     dma = pltpu.SemaphoreType.DMA
     vmem = pl.BlockSpec(memory_space=pltpu.VMEM)
-    smem = pl.BlockSpec(memory_space=pltpu.SMEM)
     hbm = pl.BlockSpec(memory_space=pl.ANY)
 
     inputs = (
@@ -625,10 +658,12 @@
         ("jac_h", jacobian_weight.T, hbm),
         ("conf_h", confidence_weight.T, hbm),
     )
+    cam_rows, cam_cols = frames * n_edge * 6 // n_tile, frames * 6
+    places = (n_edge, cam_rows + cam_cols, 128)
     outputs = (
         ("out_hidden", (edges, band, chan), BF, hbm),
         ("gall", (n_edge, 16, 128), F32, vmem),
-        ("meta_all", (n_edge, 1, 128), jnp.int32, hbm),
+        ("where_h", places, BF, hbm),
     )
     near, far = len(reach(NEAR, rows)), len(reach(FAR, rows))
     scratch = {
@@ -644,6 +679,11 @@
         "meta_s": pltpu.SMEM((n_edge, 1, 128), jnp.int32),
         "feat": pltpu.VMEM((frames, band, chan), BF),
         "held": pltpu.VMEM((edges, band, chan), BF),
+        "ready": pltpu.VMEM((edges, band, chan), BF),
+        "where_v": pltpu.VMEM(places, BF),
+        "raw_s": pltpu.SMEM((2, n_edge, edges), jnp.int32),
+        "s_raw": pltpu.SemaphoreType.DMA((2, n_edge - 1)),
+        "r_raw": pltpu.SemaphoreType.DMA((2, n_edge - 1)),
         "send": pltpu.VMEM(((n_edge - 1) * slots, band, chan), BF),
         "text": pltpu.VMEM((edges, (even + 2 * RADIUS + 3) // 4 * 4 * width, chan), BF),
         "sext": pltpu.VMEM((edges, even * width, chan), BF),
@@ -685,7 +725,7 @@
             scratch[f"s_{key}{way}"] = dma((count,))
             scratch[f"r_{key}{way}"] = dma((count, lots))
     names = [i[0] for i in inputs] + [o[0] for o in outputs] + list(scratch)
-    state, gall, meta_all = pl.pallas_call(
+    state, gall, where = pl.pallas_call(
         functools.partial(kernel, dims, names),
         out_shape=tuple(jax.ShapeDtypeStruct(shape, kind) for _, shape, kind, _ in outputs),
         in_specs=[spec for _, _, spec in inputs],
@@ -699,13 +739,13 @@
         functools.partial(assemble, dims),
         out_shape=(
             jax.ShapeDtypeStruct((edges, band, chan), BF),
-            jax.ShapeDtypeStruct((frames * n_edge * 6 // n_tile, frames * 6), F32),
+            jax.ShapeDtypeStruct((cam_rows, cam_cols), F32),
             jax.ShapeDtypeStruct((frames, 36), F32),
         ),
-        in_specs=[smem, vmem, hbm],
+        in_specs=[vmem, vmem, hbm],
         out_specs=(hbm, vmem, vmem),
         scratch_shapes=[pltpu.VMEM((edges, band, chan), BF), dma((2,))],
-    )(meta_all, gall, state)
+    )(where, gall, state)
     return hidden_next.reshape(hidden_state.shape), cam, diag
 
 

time: 47.5 us -> 54.7 us (1.15)
  Pallas kernels: 45.9 us -> 53.3 us
    pallas_call x1, Pallas kernels: 42.4 us -> 49.7 us  [per_device(): pl.pallas_call(functools.partial(kernel, dims, names), out_shape=tuple((j...]
where the time goes in v6:
time: 54.7 us; the launch traced here: 54.6 us
  Pallas kernels  53.3 us (97%)
  between operations  1.29 us (2%)
    pallas_call x1, Pallas kernels, per_device(): pl.pallas_call(functools.partial(kernel, dims, names), out_shape=tuple((j...  49.7 us
    pallas_call x1, Pallas kernels, per_device(): pl.pallas_call(functools.partial(assemble, dims), out_shape=(jax.ShapeDty...  3.61 us

profile of v6, /device:TPU:0, one launch (start us, length us, event | category | flops | bytes accessed | tf_op | source)
XLA Modules:
  0.0 54.6 jit_solution(13735544004215304950)
XLA Ops:
  1.3 49.7 %shard_map.130 = (bf16[8,384,128]{2,1,0:T(8,128)(2,1)}, f32[4,16,128]{2,1,0:T(8,128)}, bf16[4,216,128]{2,1,0:T(8,128)(2,1)}) custom-call(s32[8]{0:T(128)} %bitcast.9, s32[8]{0:T(128)} %refs_1_.1, s32[8]{0:T(128)} %refs_2_.1, s32[1]{0:T(128)S(6)} %copy.14.refs_3_, bf16[24,384,128]{2,1,0:T(8,128)(2,1)} %bitcast.6, bf16[8,384,128]{2,1,0:T(8,128)(2,1)} %bitcast.7, ...), custom_call_target="tpu_custom_call" | custom-call | tf_op jit(solution)/shard_map/pallas_call | solution.py:728
  50.9 3.6 %shard_map.131 = (bf16[8,384,128]{2,1,0:T(8,128)(2,1)}, f32[72,144]{1,0:T(8,128)}, f32[24,36]{1,0:T(8,128)}) custom-call(bf16[4,216,128]{2,1,0:T(8,128)(2,1)} %get-tuple-element.9.where_v, f32[4,16,128]{2,1,0:T(8,128)} %get-tuple-element.10.gall, bf16[8,384,128]{2,1,0:T(8,128)(2,1)} %get-tuple-element.11.hidden_h), custom_call_target="tpu_custom_call" | custom-call | tf_op jit(solution)/shard_map/pallas_call | solution.py:738

commit v7 on v5

--- a/solution.py
+++ b/solution.py
@@ -13,7 +13,8 @@
 RADIUS = WINDOW // 2
 NEAR = 2
 FAR = RADIUS + NEAR
-OWNER, TARGET, SOURCE, PLACE, GROUP, REL, ASKS = 0, 8, 16, 32, 40, 48, 64
+OWNER, TARGET, SOURCE, SPOT, PLACE, GROUP, REL, ASKS = 0, 8, 16, 24, 32, 40, 48, 64
+PIECES = 4
 MESH = pl.DeviceIdType.MESH
 BF = jnp.bfloat16
 F32 = jnp.float32
@@ -132,6 +133,7 @@
         )
         for base, value in fields:
             row = jnp.where(lane == base + spot, value, row)
+        row = jnp.where(lane == SPOT + e, spot, row)
         row = jnp.where(lane == ASKS + rel_of[e] * slots + rank[e], goal, row)
     r.row_v[...] = row
     mine = pltpu.make_async_copy(r.row_v, r.row_s, r.l_row)
@@ -155,8 +157,11 @@
             (me + rel) % n_edge, tile,
         )
 
+    others = n_edge - 1
     for rel in range(1, n_edge):
         meta_copy(rel).start()
+    own_row = pltpu.make_async_copy(r.row_v, r.meta_s.at[me], r.l_own)
+    own_row.start()
 
     class Halo:
         def __init__(self, halo, lot, buf, source, sems):
@@ -238,8 +243,6 @@
     txt = Halo(FAR, 1, r.text, inner(r.text, FAR), (r.s_tup, r.r_tup, r.s_tdn, r.r_tdn))
 
     hid.start(0)
-    own_row = pltpu.make_async_copy(r.row_v, r.meta_s.at[me], r.l_own)
-    own_row.start()
     for rel in range(1, n_edge):
         remote(
             r.row_v, r.meta_s.at[(me - rel + n_edge) % n_edge], r.s_meta.at[rel - 1],
@@ -247,8 +250,6 @@
         ).wait_recv()
     loads[0].wait()
 
-    others = n_edge - 1
-
     def feat_copy(rel, s):
         return remote(
             r.send.at[s * others + rel - 1], texts[s].at[rel - 1],
@@ -269,9 +270,6 @@
             feat_copy(rel, s).start()
 
     mine.wait()
-    own_row.wait()
-    tables = pltpu.make_async_copy(r.meta_s, r.meta_all, r.l_meta)
-    tables.start()
 
     def take_source(e):
         r.sext[e, pl.ds(NEAR * width, band)] = r.feat[r.row_s[0, SOURCE + e]]
@@ -369,6 +367,27 @@
     take(0)
     each(slots - slots // 2, lambda p: state_part(p + slots // 2))
     src.received(0)
+
+    own_row.wait()
+    cam_cols = frames * 6
+    cam_rows = r.where_v.shape[1] - cam_cols
+    part = iota((cam_rows + cam_cols, 128), 0)
+    index = jnp.where(part < cam_rows, part + tile * cam_rows, part - cam_rows + me * cam_cols)
+    inside = lane & 15
+    digit = jnp.where(inside < 6, inside, inside - 6)
+
+    def place(j):
+        spots = jnp.full((1, 128), -1, jnp.int32)
+        for e in range(edges):
+            source = (j * frames + r.meta_s[j, 0, SOURCE + e]) * 6
+            target = (r.meta_s[j, 0, OWNER + e] * frames + r.meta_s[j, 0, TARGET + e]) * 6
+            here = jnp.where(inside < 6, source, target) + digit
+            spots = jnp.where(((lane >> 4) == e) & (inside < 12), here, spots)
+        r.where_v[j] = one_hot(index == spots)
+
+    each(n_edge, place)
+    tables = pltpu.make_async_copy(r.where_v, r.where_h, r.l_meta)
+    tables.start()
 
     lane_w = (iota((width, 128), 1) + 4) & 127
     col_w = iota((width, 128), 0) + RADIUS - (lane_w & 7)
@@ -459,9 +478,6 @@
         update(p)
 
     each(slots, stage)
-    store = pltpu.make_async_copy(r.held, r.out_hidden, r.l_out)
-    store.start()
-
     same = (iota((128, 128), 0) >> 4) == (iota((128, 128), 1) >> 4)
     square = jnp.where(same, nt(r.wall[...], r.jall[...]), 0.0)
     blocks = square[0:16]
@@ -486,6 +502,13 @@
     for rel in range(1, n_tile):
         tile_copy(rel).start()
     r.gtile[tile] = r.gpart[...]
+
+    def put_back(e):
+        r.ready[e] = r.held[r.row_s[0, SPOT + e]]
+
+    each(edges, put_back)
+    store = pltpu.make_async_copy(r.ready, r.out_hidden, r.l_out)
+    store.start()
     all_tiles().wait_recv()
     total = r.gtile[0]
     for k in range(1, n_tile):
@@ -493,17 +516,19 @@
     r.gsum[...] = total
 
     def edge_copy(rel):
-        return remote(r.gsum, r.gall.at[me], r.s_ge, r.r_ge, (me + rel) % n_edge, tile)
+        return remote(r.gsum, r.gall_h.at[me], r.s_ge, r.r_ge, (me + rel) % n_edge, tile)
 
     def all_edges():
-        some = r.gall.at[pl.ds(0, others)]
+        some = r.gall_h.at[pl.ds(0, others)]
         return remote(some, some, r.s_ge, r.r_ge, (me + 1) % n_edge, tile)
 
     for rel in range(1, n_edge):
         edge_copy(rel).start()
-    r.gall[me] = total
+    own_sum = pltpu.make_async_copy(r.gsum, r.gall_h.at[me], r.l_sum)
+    own_sum.start()
     all_edges().wait_recv()
 
+    own_sum.wait()
     store.wait()
     tables.wait()
     for rel in range(1, n_edge):
@@ -521,29 +546,38 @@
     return high, (value - high.astype(F32)).astype(BF)
 
 
-def assemble(dims, meta_s, gall, hidden_h, out_hidden, out_cam, out_diag, held, sem):
+def assemble(
+    dims, where_h, gall_h, hidden_h, out_hidden, cam_h, diag_h, where_v, gall, out_cam, out_diag, held,
+    sem, held_sem,
+):
     n_edge, n_tile, edges, frames, rows, width, slots = dims
     me = lax.axis_index("edge")
     tile = lax.axis_index("tile")
-    fetch = pltpu.make_async_copy(hidden_h, held, sem.at[0])
-    fetch.start()
+    loads = [
+        pltpu.make_async_copy(gall_h, gall, sem.at[0]),
+        pltpu.make_async_copy(where_h, where_v, sem.at[1]),
+    ]
+    pieces = [pl.ds(i * (edges // PIECES), edges // PIECES) for i in range(PIECES)]
+    fetches = [
+        pltpu.make_async_copy(hidden_h.at[p], held.at[p], held_sem.at[i])
+        for i, p in enumerate(pieces)
+    ]
+    stores = [
+        pltpu.make_async_copy(held.at[p], out_hidden.at[p], held_sem.at[i])
+        for i, p in enumerate(pieces)
+    ]
+    for load in loads + fetches:
+        load.start()
     cam_rows, cam_cols = out_cam.shape
-    row_id = iota((cam_rows, 128), 0) + tile * cam_rows
-    col_id = iota((cam_cols, 128), 0) + me * cam_cols
     same = (iota((128, 128), 0) >> 4) == (iota((128, 128), 1) >> 4)
-    lane = iota((1, 128), 1)
-    inner = lane & 15
-    digit = jnp.where(inner < 6, inner, inner - 6)
+    for load in loads:
+        load.wait()
+    for fetch, store in zip(fetches, stores):
+        fetch.wait()
+        store.start()
     lefts, lows, rights = [], [], []
     for j in range(n_edge):
-        spots = jnp.full((1, 128), -1, jnp.int32)
-        for e in range(edges):
-            source = (j * frames + meta_s[j, 0, SOURCE + e]) * 6
-            target = (meta_s[j, 0, OWNER + e] * frames + meta_s[j, 0, TARGET + e]) * 6
-            here = jnp.where(inner < 6, source, target) + digit
-            spots = jnp.where(((lane >> 4) == e) & (inner < 12), here, spots)
-        mine = (col_id == spots).astype(F32)
-        left = jnp.concatenate([(row_id == spots).astype(F32), mine], axis=0).astype(BF)
+        left = where_v[j]
         stack = jnp.where(same, jnp.concatenate([gall[j]] * 8, axis=0), 0.0)
         picked = nn(
             jnp.concatenate([left, left], axis=1), jnp.concatenate(halves(stack), axis=0)
@@ -551,19 +585,14 @@
         high, low = halves(picked)
         lefts.append(high)
         lows.append(low)
-        rights.append(mine.astype(BF))
+        rights.append(left[cam_rows:])
     placed = nt(jnp.concatenate(lefts + lows, axis=1), jnp.concatenate(rights + rights, axis=1))
-    fetch.wait()
-    stores = [
-        pltpu.make_async_copy(held.at[e], out_hidden.at[meta_s[me, 0, PLACE + e]], sem.at[1])
-        for e in range(edges)
-    ]
-    for store in stores:
-        store.start()
     cam = placed[0:cam_rows]
     row_frame = sixth(iota((cam_rows, cam_cols), 0) + tile * cam_rows)
     col_frame = sixth(iota((cam_rows, cam_cols), 1) + me * cam_cols)
     out_cam[...] = jnp.where(row_frame == col_frame, 0.0, cam)
+    cam_store = pltpu.make_async_copy(out_cam, cam_h, sem.at[0])
+    cam_store.start()
     own = placed[cam_rows:]
     own_row = sixth(iota((cam_cols, cam_cols), 0))
     own_col = sixth(iota((cam_cols, cam_cols), 1))
@@ -581,7 +610,10 @@
     )
     high, low = halves(spread)
     out_diag[...] = (nn(fold, high) + nn(fold, low))[:, 0:36]
-    pltpu.make_async_copy(held, out_hidden, sem.at[1]).wait()
+    diag_store = pltpu.make_async_copy(out_diag, diag_h, sem.at[1])
+    diag_store.start()
+    for store in stores + [cam_store, diag_store]:
+        store.wait()
 
 
 def per_device(
@@ -608,8 +640,6 @@
     dims = (n_edge, n_tile, edges, frames, rows, width, slots)
     even = (rows + 2 * NEAR + 1) // 2 * 2
     dma = pltpu.SemaphoreType.DMA
-    vmem = pl.BlockSpec(memory_space=pltpu.VMEM)
-    smem = pl.BlockSpec(memory_space=pltpu.SMEM)
     hbm = pl.BlockSpec(memory_space=pl.ANY)
 
     inputs = (
@@ -625,10 +655,12 @@
         ("jac_h", jacobian_weight.T, hbm),
         ("conf_h", confidence_weight.T, hbm),
     )
+    cam_rows, cam_cols = frames * n_edge * 6 // n_tile, frames * 6
+    places = (n_edge, cam_rows + cam_cols, 128)
     outputs = (
         ("out_hidden", (edges, band, chan), BF, hbm),
-        ("gall", (n_edge, 16, 128), F32, vmem),
-        ("meta_all", (n_edge, 1, 128), jnp.int32, hbm),
+        ("gall_h", (n_edge, 16, 128), F32, hbm),
+        ("where_h", places, BF, hbm),
     )
     near, far = len(reach(NEAR, rows)), len(reach(FAR, rows))
     scratch = {
@@ -644,6 +676,8 @@
         "meta_s": pltpu.SMEM((n_edge, 1, 128), jnp.int32),
         "feat": pltpu.VMEM((frames, band, chan), BF),
         "held": pltpu.VMEM((edges, band, chan), BF),
+        "ready": pltpu.VMEM((edges, band, chan), BF),
+        "where_v": pltpu.VMEM(places, BF),
         "send": pltpu.VMEM(((n_edge - 1) * slots, band, chan), BF),
         "text": pltpu.VMEM((edges, (even + 2 * RADIUS + 3) // 4 * 4 * width, chan), BF),
         "sext": pltpu.VMEM((edges, even * width, chan), BF),
@@ -668,6 +702,7 @@
         "l_row": dma,
         "l_meta": dma,
         "l_own": dma,
+        "l_sum": dma,
         "l_out": dma,
         "s_meta": dma((n_edge - 1,)),
         "r_meta": dma((n_edge - 1,)),
@@ -685,7 +720,7 @@
             scratch[f"s_{key}{way}"] = dma((count,))
             scratch[f"r_{key}{way}"] = dma((count, lots))
     names = [i[0] for i in inputs] + [o[0] for o in outputs] + list(scratch)
-    state, gall, meta_all = pl.pallas_call(
+    state, gall, where = pl.pallas_call(
         functools.partial(kernel, dims, names),
         out_shape=tuple(jax.ShapeDtypeStruct(shape, kind) for _, shape, kind, _ in outputs),
         in_specs=[spec for _, _, spec in inputs],
@@ -699,13 +734,21 @@
         functools.partial(assemble, dims),
         out_shape=(
             jax.ShapeDtypeStruct((edges, band, chan), BF),
-            jax.ShapeDtypeStruct((frames * n_edge * 6 // n_tile, frames * 6), F32),
+            jax.ShapeDtypeStruct((cam_rows, cam_cols), F32),
             jax.ShapeDtypeStruct((frames, 36), F32),
         ),
-        in_specs=[smem, vmem, hbm],
-        out_specs=(hbm, vmem, vmem),
-        scratch_shapes=[pltpu.VMEM((edges, band, chan), BF), dma((2,))],
-    )(meta_all, gall, state)
+        in_specs=[hbm] * 3,
+        out_specs=(hbm,) * 3,
+        scratch_shapes=[
+            pltpu.VMEM(places, BF),
+            pltpu.VMEM((n_edge, 16, 128), F32),
+            pltpu.VMEM((cam_rows, cam_cols), F32),
+            pltpu.VMEM((frames, 36), F32),
+            pltpu.VMEM((edges, band, chan), BF),
+            dma((2,)),
+            dma((PIECES,)),
+        ],
+    )(where, gall, state)
     return hidden_next.reshape(hidden_state.shape), cam, diag
 
 

time: 47.5 us -> 46.2 us (0.973)
  Pallas kernels: 45.9 us -> 44.8 us
    pallas_call x1, Pallas kernels: 3.53 us -> 2.81 us  [per_device(): pl.pallas_call(functools.partial(assemble, dims), out_shape=(jax.ShapeDty...]
where the time goes in v7:
time: 46.2 us; the launch traced here: 46.1 us
  Pallas kernels  44.8 us (97%)
  between operations  1.29 us (3%)
    pallas_call x1, Pallas kernels, per_device(): pl.pallas_call(functools.partial(kernel, dims, names), out_shape=tuple((j...  42 us
    pallas_call x1, Pallas kernels, per_device(): pl.pallas_call(functools.partial(assemble, dims), out_shape=(jax.ShapeDty...  2.81 us

profile of v7, /device:TPU:0, one launch (start us, length us, event | category | flops | bytes accessed | tf_op | source)
XLA Modules:
  0.0 46.1 jit_solution(3174988874081079790)
XLA Ops:
  1.3 42.0 %shard_map.130 = (bf16[8,384,128]{2,1,0:T(8,128)(2,1)}, f32[4,16,128]{2,1,0:T(8,128)}, bf16[4,216,128]{2,1,0:T(8,128)(2,1)}) custom-call(s32[8]{0:T(128)} %bitcast.9, s32[8]{0:T(128)} %refs_1_.1, s32[8]{0:T(128)} %refs_2_.1, s32[1]{0:T(128)S(6)} %copy.14.refs_3_, bf16[24,384,128]{2,1,0:T(8,128)(2,1)} %bitcast.6, bf16[8,384,128]{2,1,0:T(8,128)(2,1)} %bitcast.7, ...), custom_call_target="tpu_custom_call" | custom-call | tf_op jit(solution)/shard_map/pallas_call | solution.py:723
  43.3 2.8 %shard_map.131 = (bf16[8,384,128]{2,1,0:T(8,128)(2,1)}, f32[72,144]{1,0:T(8,128)}, f32[24,36]{1,0:T(8,128)}) custom-call(bf16[4,216,128]{2,1,0:T(8,128)(2,1)} %get-tuple-element.9.where_h, f32[4,16,128]{2,1,0:T(8,128)} %get-tuple-element.10.gall_h, bf16[8,384,128]{2,1,0:T(8,128)(2,1)} %get-tuple-element.11.hidden_h), custom_call_target="tpu_custom_call" | custom-call | tf_op jit(solution)/shard_map/pallas_call | solution.py:733

commit v8 on v7

--- a/solution.py
+++ b/solution.py
@@ -89,7 +89,7 @@
                 )
             )
     filled = fills[:2] + [pltpu.make_async_copy(r.wc, r.wc, r.l_w.at[2])]
-    for load in ints + loads + fills:
+    for load in ints:
         load.start()
 
     barrier = pltpu.get_barrier_semaphore()
@@ -101,6 +101,9 @@
         pl.semaphore_signal(
             barrier, inc=1, device_id=(me, (tile + rel) % n_tile), device_id_type=MESH
         )
+
+    for load in loads + fills:
+        load.start()
 
     for load in ints:
         load.wait()
@@ -240,15 +243,13 @@
     src = Halo(
         NEAR, edges, r.sext, inner(r.sext, NEAR), (r.s_sup, r.r_sup, r.s_sdn, r.r_sdn)
     )
-    txt = Halo(FAR, 1, r.text, inner(r.text, FAR), (r.s_tup, r.r_tup, r.s_tdn, r.r_tdn))
-
-    hid.start(0)
-    for rel in range(1, n_edge):
-        remote(
-            r.row_v, r.meta_s.at[(me - rel + n_edge) % n_edge], r.s_meta.at[rel - 1],
-            r.r_meta.at[rel - 1], (me + rel) % n_edge, tile,
-        ).wait_recv()
+    txt = Halo(FAR, per, r.text, inner(r.text, FAR), (r.s_tup, r.r_tup, r.s_tdn, r.r_tdn))
+
     loads[0].wait()
+
+    turns = [n_edge // 2]
+    turns += [n_edge - k - (n_edge - 2 * k) * (me % 2) for k in range(1, (n_edge + 1) // 2)]
+    turns += [k + (n_edge - 2 * k) * (me % 2) for k in range(1, (n_edge + 1) // 2)]
 
     def feat_copy(rel, s):
         return remote(
@@ -263,12 +264,17 @@
         )
 
     for s in range(slots):
-        for rel in range(1, n_edge):
+        for rel in turns:
             peer = (me - rel + n_edge) % n_edge
+            if s == 0:
+                remote(
+                    r.row_v, r.meta_s.at[peer], r.s_meta.at[rel - 1], r.r_meta.at[rel - 1],
+                    (me + rel) % n_edge, tile,
+                ).wait_recv()
             r.send[s * others + rel - 1] = r.feat[r.meta_s[peer, 0, ASKS + rel * slots + s]]
-        for rel in range(1, n_edge):
             feat_copy(rel, s).start()
 
+    hid.start(0)
     mine.wait()
 
     def take_source(e):
@@ -355,12 +361,12 @@
             r.text[e, pl.ds(FAR * width + first, count)] = nn(
                 flip[0:count, 0:count], value[first : first + count]
             ).astype(BF)
-        txt.start(e)
 
     def take(s):
         feat_group(s).wait_recv()
         for q in range(per):
             take_target(s * per + q, s)
+        txt.start(s)
 
     hid.received(0)
     each(slots // 2, state_part)
@@ -428,8 +434,8 @@
         spread(jnp.maximum(value[0:used_rows], 0.0), r.x3.at[q])
 
     def update(p):
+        txt.received(p)
         for q in range(per):
-            txt.received(p * per + q)
             motion_of(p * per + q, q)
         for q in range(per):
             e = p * per + q
@@ -715,7 +721,7 @@
     }
     for s in range(slots):
         scratch[f"text{s}"] = pltpu.VMEM((n_edge - 1, band, chan), BF)
-    for key, count, lots in (("h", near, 1), ("s", near, 1), ("t", far, edges)):
+    for key, count, lots in (("h", near, 1), ("s", near, 1), ("t", far, slots)):
         for way in ("up", "dn"):
             scratch[f"s_{key}{way}"] = dma((count,))
             scratch[f"r_{key}{way}"] = dma((count, lots))

time: 46.2 us -> 45.6 us (0.987)
  Pallas kernels: 44.8 us -> 44.2 us
    pallas_call x1, Pallas kernels: 42 us -> 41.3 us  [per_device(): pl.pallas_call(functools.partial(kernel, dims, names), out_shape=tuple((j...]
where the time goes in v8:
time: 45.6 us; the launch traced here: 45.4 us
  Pallas kernels  44.2 us (97%)
  between operations  1.29 us (3%)
    pallas_call x1, Pallas kernels, per_device(): pl.pallas_call(functools.partial(kernel, dims, names), out_shape=tuple((j...  41.3 us
    pallas_call x1, Pallas kernels, per_device(): pl.pallas_call(functools.partial(assemble, dims), out_shape=(jax.ShapeDty...  2.81 us

profile of v8, /device:TPU:0, one launch (start us, length us, event | category | flops | bytes accessed | tf_op | source)
XLA Modules:
  0.0 45.4 jit_solution(1987764521318507720)
XLA Ops:
  1.3 41.3 %shard_map.130 = (bf16[8,384,128]{2,1,0:T(8,128)(2,1)}, f32[4,16,128]{2,1,0:T(8,128)}, bf16[4,216,128]{2,1,0:T(8,128)(2,1)}) custom-call(s32[8]{0:T(128)} %bitcast.9, s32[8]{0:T(128)} %refs_1_.1, s32[8]{0:T(128)} %refs_2_.1, s32[1]{0:T(128)S(6)} %copy.14.refs_3_, bf16[24,384,128]{2,1,0:T(8,128)(2,1)} %bitcast.6, bf16[8,384,128]{2,1,0:T(8,128)(2,1)} %bitcast.7, ...), custom_call_target="tpu_custom_call" | custom-call | tf_op jit(solution)/shard_map/pallas_call | solution.py:729
  42.6 2.8 %shard_map.131 = (bf16[8,384,128]{2,1,0:T(8,128)(2,1)}, f32[72,144]{1,0:T(8,128)}, f32[24,36]{1,0:T(8,128)}) custom-call(bf16[4,216,128]{2,1,0:T(8,128)(2,1)} %get-tuple-element.9.where_h, f32[4,16,128]{2,1,0:T(8,128)} %get-tuple-element.10.gall_h, bf16[8,384,128]{2,1,0:T(8,128)(2,1)} %get-tuple-element.11.hidden_h), custom_call_target="tpu_custom_call" | custom-call | tf_op jit(solution)/shard_map/pallas_call | solution.py:739

commit v9 on v8

--- a/solution.py
+++ b/solution.py
@@ -437,7 +437,6 @@
         txt.received(p)
         for q in range(per):
             motion_of(p * per + q, q)
-        for q in range(per):
             e = p * per + q
             before = r.gpre[e] + nn(windows(r.x3, q, rows + 2), r.wm[...].reshape(9 * 128, 256))
             r.upd[q] = 0.5 * jnp.tanh(0.5 * before[width : width + band, 0:128]) + 0.5

time: 45.6 us -> 45.5 us (level)
  no operation moved by 1% of the time
where the time goes in v9:
time: 45.5 us; the launch traced here: 45.3 us
  Pallas kernels  44 us (97%)
  between operations  1.29 us (3%)
    pallas_call x1, Pallas kernels, per_device(): pl.pallas_call(functools.partial(kernel, dims, names), out_shape=tuple((j...  41.2 us
    pallas_call x1, Pallas kernels, per_device(): pl.pallas_call(functools.partial(assemble, dims), out_shape=(jax.ShapeDty...  2.81 us

profile of v9, /device:TPU:0, one launch (start us, length us, event | category | flops | bytes accessed | tf_op | source)
XLA Modules:
  0.0 45.3 jit_solution(17541652153960915307)
XLA Ops:
  1.3 41.2 %shard_map.130 = (bf16[8,384,128]{2,1,0:T(8,128)(2,1)}, f32[4,16,128]{2,1,0:T(8,128)}, bf16[4,216,128]{2,1,0:T(8,128)(2,1)}) custom-call(s32[8]{0:T(128)} %bitcast.9, s32[8]{0:T(128)} %refs_1_.1, s32[8]{0:T(128)} %refs_2_.1, s32[1]{0:T(128)S(6)} %copy.14.refs_3_, bf16[24,384,128]{2,1,0:T(8,128)(2,1)} %bitcast.6, bf16[8,384,128]{2,1,0:T(8,128)(2,1)} %bitcast.7, ...), custom_call_target="tpu_custom_call" | custom-call | tf_op jit(solution)/shard_map/pallas_call | solution.py:728
  42.5 2.8 %shard_map.131 = (bf16[8,384,128]{2,1,0:T(8,128)(2,1)}, f32[72,144]{1,0:T(8,128)}, f32[24,36]{1,0:T(8,128)}) custom-call(bf16[4,216,128]{2,1,0:T(8,128)(2,1)} %get-tuple-element.9.where_h, f32[4,16,128]{2,1,0:T(8,128)} %get-tuple-element.10.gall_h, bf16[8,384,128]{2,1,0:T(8,128)(2,1)} %get-tuple-element.11.hidden_h), custom_call_target="tpu_custom_call" | custom-call | tf_op jit(solution)/shard_map/pallas_call | solution.py:738

commit v10 on v8

--- a/solution.py
+++ b/solution.py
@@ -494,7 +494,7 @@
     for e in range(edges):
         used = (r.row_s[0, PLACE + e] < r.count_s[0]).astype(jnp.int32)
         blocks = jnp.where((of == e) & (jnp.full((16, 128), used) == 0), 0.0, blocks)
-    r.gpart[...] = blocks
+    r.gpart[...] = blocks.astype(BF)
 
     def tile_copy(rel):
         return remote(
@@ -516,9 +516,9 @@
     store = pltpu.make_async_copy(r.ready, r.out_hidden, r.l_out)
     store.start()
     all_tiles().wait_recv()
-    total = r.gtile[0]
+    total = r.gtile[0].astype(F32)
     for k in range(1, n_tile):
-        total = total + r.gtile[k]
+        total = total + r.gtile[k].astype(F32)
     r.gsum[...] = total
 
     def edge_copy(rel):
@@ -699,8 +699,8 @@
         "upd": pltpu.VMEM((per, band, chan), F32),
         "jall": pltpu.VMEM((128, 2 * band), BF),
         "wall": pltpu.VMEM((128, 2 * band), BF),
-        "gpart": pltpu.VMEM((16, 128), F32),
-        "gtile": pltpu.VMEM((n_tile, 16, 128), F32),
+        "gpart": pltpu.VMEM((16, 128), BF),
+        "gtile": pltpu.VMEM((n_tile, 16, 128), BF),
         "gsum": pltpu.VMEM((16, 128), F32),
         "l_in": dma((5,)),
         "l_w": dma((3,)),

time: 45.6 us -> 45.6 us (level)
  no operation moved by 1% of the time
where the time goes in v10:
time: 45.6 us; the launch traced here: 45.4 us
  Pallas kernels  44.1 us (97%)
  between operations  1.29 us (3%)
    pallas_call x1, Pallas kernels, per_device(): pl.pallas_call(functools.partial(kernel, dims, names), out_shape=tuple((j...  41.3 us
    pallas_call x1, Pallas kernels, per_device(): pl.pallas_call(functools.partial(assemble, dims), out_shape=(jax.ShapeDty...  2.81 us

profile of v10, /device:TPU:0, one launch (start us, length us, event | category | flops | bytes accessed | tf_op | source)
XLA Modules:
  0.0 45.4 jit_solution(3574954989272327120)
XLA Ops:
  1.3 41.3 %shard_map.130 = (bf16[8,384,128]{2,1,0:T(8,128)(2,1)}, f32[4,16,128]{2,1,0:T(8,128)}, bf16[4,216,128]{2,1,0:T(8,128)(2,1)}) custom-call(s32[8]{0:T(128)} %bitcast.9, s32[8]{0:T(128)} %refs_1_.1, s32[8]{0:T(128)} %refs_2_.1, s32[1]{0:T(128)S(6)} %copy.14.refs_3_, bf16[24,384,128]{2,1,0:T(8,128)(2,1)} %bitcast.6, bf16[8,384,128]{2,1,0:T(8,128)(2,1)} %bitcast.7, ...), custom_call_target="tpu_custom_call" | custom-call | tf_op jit(solution)/shard_map/pallas_call | solution.py:729
  42.6 2.8 %shard_map.131 = (bf16[8,384,128]{2,1,0:T(8,128)(2,1)}, f32[72,144]{1,0:T(8,128)}, f32[24,36]{1,0:T(8,128)}) custom-call(bf16[4,216,128]{2,1,0:T(8,128)(2,1)} %get-tuple-element.9.where_h, f32[4,16,128]{2,1,0:T(8,128)} %get-tuple-element.10.gall_h, bf16[8,384,128]{2,1,0:T(8,128)(2,1)} %get-tuple-element.11.hidden_h), custom_call_target="tpu_custom_call" | custom-call | tf_op jit(solution)/shard_map/pallas_call | solution.py:739

commit v11 on v9

--- a/solution.py
+++ b/solution.py
@@ -577,9 +577,6 @@
     same = (iota((128, 128), 0) >> 4) == (iota((128, 128), 1) >> 4)
     for load in loads:
         load.wait()
-    for fetch, store in zip(fetches, stores):
-        fetch.wait()
-        store.start()
     lefts, lows, rights = [], [], []
     for j in range(n_edge):
         left = where_v[j]
@@ -592,6 +589,9 @@
         lows.append(low)
         rights.append(left[cam_rows:])
     placed = nt(jnp.concatenate(lefts + lows, axis=1), jnp.concatenate(rights + rights, axis=1))
+    for fetch, store in zip(fetches, stores):
+        fetch.wait()
+        store.start()
     cam = placed[0:cam_rows]
     row_frame = sixth(iota((cam_rows, cam_cols), 0) + tile * cam_rows)
     col_frame = sixth(iota((cam_rows, cam_cols), 1) + me * cam_cols)

time: 45.5 us -> 45.5 us (level)
  no operation moved by 1% of the time
where the time goes in v11:
time: 45.5 us; the launch traced here: 45.3 us
  Pallas kernels  44 us (97%)
  between operations  1.29 us (3%)
    pallas_call x1, Pallas kernels, per_device(): pl.pallas_call(functools.partial(kernel, dims, names), out_shape=tuple((j...  41.2 us
    pallas_call x1, Pallas kernels, per_device(): pl.pallas_call(functools.partial(assemble, dims), out_shape=(jax.ShapeDty...  2.82 us

profile of v11, /device:TPU:0, one launch (start us, length us, event | category | flops | bytes accessed | tf_op | source)
XLA Modules:
  0.0 45.3 jit_solution(16998619197024786719)
XLA Ops:
  1.3 41.2 %shard_map.130 = (bf16[8,384,128]{2,1,0:T(8,128)(2,1)}, f32[4,16,128]{2,1,0:T(8,128)}, bf16[4,216,128]{2,1,0:T(8,128)(2,1)}) custom-call(s32[8]{0:T(128)} %bitcast.9, s32[8]{0:T(128)} %refs_1_.1, s32[8]{0:T(128)} %refs_2_.1, s32[1]{0:T(128)S(6)} %copy.14.refs_3_, bf16[24,384,128]{2,1,0:T(8,128)(2,1)} %bitcast.6, bf16[8,384,128]{2,1,0:T(8,128)(2,1)} %bitcast.7, ...), custom_call_target="tpu_custom_call" | custom-call | tf_op jit(solution)/shard_map/pallas_call | solution.py:728
  42.5 2.8 %shard_map.131 = (bf16[8,384,128]{2,1,0:T(8,128)(2,1)}, f32[72,144]{1,0:T(8,128)}, f32[24,36]{1,0:T(8,128)}) custom-call(bf16[4,216,128]{2,1,0:T(8,128)(2,1)} %get-tuple-element.9.where_h, f32[4,16,128]{2,1,0:T(8,128)} %get-tuple-element.10.gall_h, bf16[8,384,128]{2,1,0:T(8,128)(2,1)} %get-tuple-element.11.hidden_h), custom_call_target="tpu_custom_call" | custom-call | tf_op jit(solution)/shard_map/pallas_call | solution.py:738
